TPU v7x, 256 devices: a whole 4x4x8 slice. The times are simulated.
256 devices in a mesh: ctx: 16 (over z, core), exp: 16 (over x, y).
Axes of the slice: x: 4, y: 4, z: 8, core: 2. Of those that a mesh axis runs over, the one named last changes fastest.
Arguments:
- query_input: bfloat16 [2048, 8192], P('ctx', 'exp'), may hold values from -6 to 6
- key_input: bfloat16 [2048, 8192], P('ctx', 'exp'), may hold values from -6 to 6
- value_input: bfloat16 [2048, 8192], P('ctx', 'exp'), may hold values from -6 to 6
- gate_logits: float32 [2, 2048, 64], P(None, 'ctx', 'exp'), may hold values from -6 to 6
- comp_weight: float32 [2, 32, 64], P(None, None, 'exp'), may hold values from -6 to 6
- out_proj: bfloat16 [8192, 7168], P('exp', 'ctx'), may hold values from -0.0625 to 0.0625
- residual_in: bfloat16 [2048, 7168], P(('ctx', 'exp')), may hold values from -3 to 3
- ffn_gain: float32 [7168], replicated, may hold values from 0.25 to 1.75
- expert_ids: int32 [2048, 2], P(('ctx', 'exp')), may hold values from 0 to 15, all different within a row; in each aligned block of 8 rows (0 to 7, 8 to 15, ...) at most 2 rows name the same one
- route_gates: float32 [2048, 2], P(('ctx', 'exp')), may hold values from 0.2 to 1
- expert_gate: bfloat16 [16, 7168, 2048], P('exp', None, 'ctx'), may hold values from -0.0625 to 0.0625
- expert_up: bfloat16 [16, 7168, 2048], P('exp', None, 'ctx'), may hold values from -0.0625 to 0.0625
- expert_down: bfloat16 [16, 2048, 7168], P('exp', 'ctx'), may hold values from -0.125 to 0.125
Outputs:
- layer_out: bfloat16 [2048, 7168], P(('ctx', 'exp'))
Inputs may be any that keep to these rules, and one draw needn't show every extreme that they name: `expert_ids`: each token names 2 different experts. In every aligned block of 8 consecutive tokens no expert is named more than 2 times, a bound that some block reaches.
All inputs are finite; a program needn't handle non-finite values.
Results may differ from a plain program's by a relative error of at most 0.0085.
Values may be sent and summed in bfloat16 or wider, within the bound.
A program may use at most 128 MiB of HBM per device.

v0:
```python
import math

import jax
import jax.numpy as jnp
from jax import lax
from jax.sharding import PartitionSpec as P

WINDOW = 512


score_gain = 2.0
norm_eps = 1e-06


def passed_along(block, axis, distance):
    devices = range(lax.axis_size(axis))
    route = [(i - distance, i) for i in devices if i - distance in devices]
    return lax.ppermute(block, axis, route)


def head_norm(matrix, head_width):
    row_count = matrix.shape[0]
    shaped = matrix.reshape(row_count, -1, head_width).astype(jnp.float32)
    scaled = shaped * lax.rsqrt(jnp.mean(shaped * shaped, axis=2, keepdims=True) + norm_eps)
    return scaled.reshape(row_count, -1)


def compress(extended, position_weights, head_width):
    stride_len = position_weights.shape[0] // 2
    head_count = position_weights.shape[1]
    blocks = extended.reshape(-1, stride_len, head_count, head_width).astype(jnp.float32)
    first_half = jnp.einsum(
        "nshd,sh->nhd", blocks[:-1], position_weights[:stride_len], precision=lax.Precision.HIGHEST
    )
    second_half = jnp.einsum(
        "nshd,sh->nhd", blocks[1:], position_weights[stride_len:], precision=lax.Precision.HIGHEST
    )
    return (first_half + second_half).reshape(blocks.shape[0] - 1, head_count * head_width)


def local(
    query_input,
    key_input,
    value_input,
    gate_logits,
    comp_weight,
    out_proj,
    residual_in,
    ffn_gain,
    expert_ids,
    route_gates,
    expert_gate,
    expert_up,
    expert_down,
):
    row_count = query_input.shape[0]
    head_count = comp_weight.shape[2]
    head_width = query_input.shape[1] // head_count
    block_len = comp_weight.shape[1]
    stride_len = block_len // 2
    exp_count = lax.axis_size("exp")
    ctx_index = lax.axis_index("ctx")
    scale = score_gain / math.sqrt(head_width)
    query_norm = head_norm(query_input, head_width).astype(jnp.bfloat16)
    key_norm = head_norm(key_input, head_width).astype(jnp.bfloat16)
    next_keys, next_values = passed_along(
        (key_input[:stride_len], value_input[:stride_len]), "ctx", -1
    )
    comp_keys = head_norm(
        compress(jnp.concatenate([key_input, next_keys], 0), comp_weight[0], head_width), head_width
    ).astype(jnp.bfloat16)
    comp_values = compress(
        jnp.concatenate([value_input, next_values], 0), comp_weight[1], head_width
    ).astype(jnp.bfloat16)
    query_pos = ctx_index * row_count + jnp.arange(row_count, dtype=jnp.int32)
    query_heads = query_norm.reshape(row_count, head_count, head_width)
    part_keys = lax.all_gather(comp_keys, "ctx", axis=0, tiled=True)
    part_values = lax.all_gather(comp_values, "ctx", axis=0, tiled=True)
    part_count = part_keys.shape[0]
    scores = jnp.einsum(
        "thd,nhd->htn",
        query_heads,
        part_keys.reshape(part_count, head_count, head_width),
        preferred_element_type=jnp.float32,
    )
    block_end = jnp.arange(part_count, dtype=jnp.int32) * stride_len + block_len - 1
    visible = block_end[None, :] <= query_pos[:, None]
    weights = jnp.where(visible[None], jnp.exp(scale * scores), 0.0)
    running_total = jnp.sum(weights, axis=2).T
    collected = jnp.einsum(
        "htn,nhd->thd",
        weights.astype(jnp.bfloat16),
        part_values.reshape(part_count, head_count, head_width),
        preferred_element_type=jnp.float32,
    )
    cmp_sum = collected.reshape(row_count, -1)
    no_block = (query_pos < block_len - 1).astype(jnp.float32)
    cmp_out = (
        cmp_sum.reshape(row_count, head_count, head_width)
        / (running_total + no_block[:, None])[:, :, None]
    )
    shift_count = max(1, WINDOW // row_count)
    earlier_keys = []
    earlier_values = []
    for distance in range(shift_count, 0, -1):
        moved_keys, moved_values = passed_along((key_norm, value_input), "ctx", distance)
        earlier_keys.append(moved_keys)
        earlier_values.append(moved_values)
    near_keys = jnp.concatenate(earlier_keys + [key_norm], 0)
    near_values = jnp.concatenate(earlier_values + [value_input], 0)
    key_pos = ctx_index * row_count - WINDOW + jnp.arange(near_keys.shape[0], dtype=jnp.int32)
    near_scores = jnp.einsum(
        "thd,shd->hts",
        query_heads,
        near_keys.reshape(-1, head_count, head_width),
        preferred_element_type=jnp.float32,
    )
    inside = (
        (key_pos[None, :] <= query_pos[:, None])
        & (key_pos[None, :] > query_pos[:, None] - WINDOW)
        & (key_pos[None, :] >= 0)
    )
    near_weights = jnp.where(inside[None], jnp.exp(scale * near_scores), 0.0)
    win_total = jnp.sum(near_weights, axis=2).T
    win_sum = jnp.einsum(
        "hts,shd->thd",
        near_weights.astype(jnp.bfloat16),
        near_values.reshape(-1, head_count, head_width),
        preferred_element_type=jnp.float32,
    )
    win_out = win_sum / win_total[:, :, None]
    branch_gates = jax.nn.sigmoid(gate_logits)
    attended = (
        (branch_gates[0][:, :, None] * cmp_out + branch_gates[1][:, :, None] * win_out)
        .reshape(row_count, -1)
        .astype(jnp.bfloat16)
    )
    token_share = row_count // exp_count
    partial_sum = jnp.dot(
        attended,
        lax.all_gather(out_proj, "ctx", axis=1, tiled=True),
        preferred_element_type=jnp.float32,
    )
    projected = lax.psum_scatter(partial_sum, "exp", scatter_dimension=0, tiled=True)
    hidden_state = residual_in.astype(jnp.float32) + projected
    mean_square = jnp.mean(hidden_state * hidden_state, axis=1, keepdims=True)
    normed = (hidden_state * lax.rsqrt(mean_square + norm_eps) * ffn_gain).astype(jnp.bfloat16)
    model_width = normed.shape[1]
    top_count = expert_ids.shape[1]
    capacity = max(2, 2 * token_share * top_count // exp_count)
    flat_ids = expert_ids.reshape(-1)
    chosen = (flat_ids[:, None] == jnp.arange(exp_count, dtype=jnp.int32)[None, :]).astype(
        jnp.int32
    )
    slots = jnp.sum((jnp.cumsum(chosen, axis=0) - chosen) * chosen, axis=1)
    targets = (flat_ids * capacity + slots).reshape(token_share, top_count)
    slot_range = jnp.arange(exp_count * capacity, dtype=jnp.int32)
    dispatch_map = jnp.sum(
        (slot_range[:, None, None] == targets[None, :, :]).astype(jnp.float32), axis=2
    ).astype(jnp.bfloat16)
    outgoing = (
        jnp.dot(dispatch_map, normed, preferred_element_type=jnp.float32)
        .astype(jnp.bfloat16)
        .reshape(exp_count, capacity, model_width)
    )
    arrived = lax.all_to_all(outgoing, "exp", split_axis=0, concat_axis=0, tiled=True)
    gate_cols = expert_gate[0]
    up_cols = expert_up[0]
    down_rows = expert_down[0]
    portion = lax.all_gather(arrived, "ctx", axis=0, tiled=True)
    flat_rows = portion.reshape(-1, model_width)
    gate_part = jnp.dot(flat_rows, gate_cols, preferred_element_type=jnp.float32)
    up_part = jnp.dot(flat_rows, up_cols, preferred_element_type=jnp.float32)
    activated = (jax.nn.silu(gate_part) * up_part).astype(jnp.bfloat16)
    partial_out = jnp.dot(activated, down_rows, preferred_element_type=jnp.float32).reshape(
        portion.shape
    )
    finished = lax.psum_scatter(
        partial_out.astype(jnp.bfloat16), "ctx", scatter_dimension=0, tiled=True
    )
    returned = lax.all_to_all(finished, "exp", split_axis=0, concat_axis=0, tiled=True).reshape(
        -1, model_width
    )
    combine_map = jnp.sum(
        jnp.where(slot_range[None, None, :] == targets[:, :, None], route_gates[:, :, None], 0.0),
        axis=1,
    )
    moe_out = jnp.dot(combine_map, returned.astype(jnp.float32), precision=lax.Precision.HIGHEST)
    return (hidden_state + moe_out).astype(jnp.bfloat16)


def solution(mesh):
    in_specs = (
        P("ctx", "exp"),
        P("ctx", "exp"),
        P("ctx", "exp"),
        P(None, "ctx", "exp"),
        P(None, None, "exp"),
        P("exp", "ctx"),
        P(("ctx", "exp"), None),
        P(),
        P(("ctx", "exp"), None),
        P(("ctx", "exp"), None),
        P("exp", None, "ctx"),
        P("exp", None, "ctx"),
        P("exp", "ctx", None),
    )
    out_specs = P(("ctx", "exp"), None)
    return jax.shard_map(local, mesh=mesh, in_specs=in_specs, out_specs=out_specs, check_vma=False)
```

profile of v0, /device:TPU:32, one launch (start us, length us, event | category | flops | bytes accessed | tf_op | source)
XLA Modules:
  0.0 410.2 jit_solution(15140837322775450915)
XLA Ops:
  8.4 5.2 %collective-permute-start.6 = (bf16[128,512]{0,1:T(8,128)(2,1)S(1)}, bf16[128,512]{0,1:T(8,128)(2,1)S(1)}, u32[]{:S(2)}, u32[]{:S(2)}) collective-permute-start(bf16[128,512]{0,1:T(8,128)(2,1)S(1)} %fusion.24), channel_id=1, source_target_pairs={{0,64},{16,80},{32,96},{48,112},{64,128},{80,144},{96,160},{112,17... | collective-permute-start | bytes 393224 | tf_op jit(solution)/shard_map/ppermute | solution.py:18
  13.6 4.2 %collective-permute-start.7 = (bf16[128,512]{0,1:T(8,128)(2,1)S(1)}, bf16[128,512]{0,1:T(8,128)(2,1)S(1)}, u32[]{:S(2)}, u32[]{:S(2)}) collective-permute-start(bf16[128,512]{0,1:T(8,128)(2,1)S(1)} %fusion.24), channel_id=1, source_target_pairs={{0,48},{16,64},{32,80},{48,96},{64,112},{80,128},{96,144},{112,160... | collective-permute-start | bytes 393224 | tf_op jit(solution)/shard_map/ppermute | solution.py:18
  17.8 2.9 collective-permute-start.8
  20.8 3.4 collective-permute-start.2
  24.2 1.3 slice.74
  25.5 3.4 collective-permute-start.1
  28.9 1.6 slice.71
  34.0 1.4 fusion.49
  39.1 1.4 collective-permute-start.3
  41.0 18.3 %all_gather.13 = bf16[128,512]{1,0:T(8,128)(2,1)S(1)} all-gather(bf16[8,512]{1,0:T(8,128)(2,1)S(1)} %fusion.45), channel_id=1, replica_groups=mesh['ctx'=16,'exp'=16] {'ctx'}, dimensions={0}, use_global_device_ids=true | all-gather | bytes 139264 | tf_op jit(solution)/shard_map/all_gather | solution.py:77
  60.4 3.2 collective-permute-start.4
  63.6 2.0 collective-permute-start.5
  65.6 5.6 %collective-permute-done.4 = bf16[128,512]{1,0:T(8,128)(2,1)S(1)} collective-permute-done((bf16[128,512]{1,0:T(8,128)(2,1)S(1)}, bf16[128,512]{1,0:T(8,128)(2,1)S(1)}, u32[]{:S(2)}, u32[]{:S(2)}) %collective-permute-start.4) | collective-permute-done | bytes 131104 | tf_op jit(solution)/shard_map/ppermute | solution.py:18
  71.2 1.9 collective-permute-start.9
  74.2 2.6 collective-permute-start
  76.8 1.6 collective-permute-done
  80.2 18.8 %all_gather.12 = bf16[128,512]{1,0:T(8,128)(2,1)S(1)} all-gather(bf16[8,512]{1,0:T(8,128)(2,1)S(1)} %fusion.44), channel_id=1, replica_groups=mesh['ctx'=16,'exp'=16] {'ctx'}, dimensions={0}, use_global_device_ids=true | all-gather | bytes 139264 | tf_op jit(solution)/shard_map/all_gather | solution.py:78
  100.2 1.6 constant_dynamic-update-slice_fusion.6
  102.4 1.7 fusion.50
  104.7 7.5 %fusion.52 = f32[128,7168]{1,0:T(8,128)} fusion(bf16[128,512]{0,1:T(8,128)(2,1)S(1)} %bitcast.126, bf16[512,7168]{0,1:T(8,128)(2,1)} %all-gather.3.cloned.1.call-done), kind=kOutput, calls=%fused_computation.101 | convolution fusion | flops 939524096 | bytes 11141120 | tf_op jit(solution)/shard_map/dot_general | solution.py:139
  114.9 107.6 %all-reduce.3.cloned.1.call-done = f32[128,7168]{1,0:T(8,128)} async-done(((f32[128,7168]{1,0:T(8,128)}), f32[128,7168]{1,0:T(8,128)}) %all-reduce.3.cloned.1.call-update) | async-done | bytes 3670032
  225.1 15.4 %all_to_all.10 = bf16[16,2,7168]{2,1,0:T(2,128)(2,1)} all-to-all(bf16[16,2,7168]{2,1,0:T(2,128)(2,1)S(1)} %reshape.231), channel_id=1, replica_groups=mesh['ctx'=16,'exp'=16] {'exp'}, dimensions={0} | all-to-all | bytes 917504 | tf_op jit(solution)/shard_map/all_to_all | solution.py:166
  240.7 47.3 %all-gather.5.cloned.1.call-done = bf16[256,2,7168]{2,1,0:T(2,128)(2,1)} async-done(((bf16[16,2,7168]{2,1,0:T(2,128)(2,1)}), bf16[256,2,7168]{2,1,0:T(2,128)(2,1)}) %all-gather.5.cloned.1.call-update) | async-done | bytes 7340048 | tf_op jit(solution)/shard_map/all_gather | solution.py:170
  288.0 15.4 %reshape.232 = bf16[512,7168]{1,0:T(8,128)(2,1)} reshape(bf16[256,2,7168]{2,1,0:T(2,128)(2,1)} %all-gather.5.cloned.1.call-done) | data formatting | bytes 14680064 | tf_op jit(solution)/shard_map/reshape | solution.py:171
  303.4 5.8 %fusion.4 = f32[512,128]{1,0:T(8,128)S(1)} fusion(bf16[512,7168]{1,0:T(8,128)(2,1)} %reshape.232, bf16[1,7168,128]{2,1,0:T(8,128)(2,1)} %param.23), kind=kOutput, calls=%fused_computation.7 | convolution fusion | flops 939524096 | bytes 9437184 | tf_op jit(solution)/shard_map/dot_general | solution.py:172
  309.6 2.1 fusion.19
  311.6 5.0 %convolution_convert_fusion = bf16[256,2,7168]{2,0,1:T(8,128)(2,1)} fusion(bf16[1,128,7168]{2,1,0:T(8,128)(2,1)S(1)} %copy-done, bf16[256,2,128]{2,1,0:T(2,128)(2,1)S(1)} %bitcast.127), kind=kOutput, calls=%fused_computation | convolution fusion | flops 943194112 | bytes 9306112 | tf_op jit(solution)/shard_map/dot_general | solution.py:175
  316.7 65.8 %reduce-scatter.2.cloned.1.call-done = bf16[16,2,7168]{2,0,1:T(8,128)(2,1)} async-done(((bf16[256,2,7168]{2,0,1:T(8,128)(2,1)}), bf16[16,2,7168]{2,0,1:T(8,128)(2,1)}) %reduce-scatter.2.cloned.1.call-update) | async-done | bytes 458768 | tf_op jit(solution)/shard_map/reduce_scatter | solution.py:178
  382.5 2.3 copy.99
  384.8 6.8 %all-to-all-start.1 = ((bf16[16,2,7168]{2,1,0:T(2,128)(2,1)}), bf16[16,2,7168]{2,1,0:T(2,128)(2,1)S(1)}, u32[]{:S(2)}, u32[]{:S(2)}) async-start(bf16[16,2,7168]{2,1,0:T(2,128)(2,1)} %copy.99), calls=%async_computation.2 | async-start | bytes 917504 | tf_op jit(solution)/shard_map/all_to_all | solution.py:181
  391.7 9.9 %all-to-all-done.1 = bf16[16,2,7168]{2,1,0:T(2,128)(2,1)S(1)} async-done(((bf16[16,2,7168]{2,1,0:T(2,128)(2,1)}), bf16[16,2,7168]{2,1,0:T(2,128)(2,1)S(1)}, u32[]{:S(2)}, u32[]{:S(2)}) %all-to-all-start.1) | async-done | bytes 458784 | tf_op jit(solution)/shard_map/all_to_all | solution.py:181
  401.8 1.9 fusion
  (114 shorter events, 21.1 us)
Async XLA Ops:
  6.5 305.1 %copy-start = (bf16[1,128,7168]{2,1,0:T(8,128)(2,1)S(1)}, bf16[1,128,7168]{2,1,0:T(8,128)(2,1)}, u32[]{:S(2)}) copy-start(bf16[1,128,7168]{2,1,0:T(8,128)(2,1)} %param.25) | copy-start | bytes 5505028
  6.5 34.0 %copy-start.2 = (bf16[128,512]{1,0:T(8,128)(2,1)S(1)}, bf16[128,512]{1,0:T(8,128)(2,1)}, u32[]{:S(2)}) copy-start(bf16[128,512]{1,0:T(8,128)(2,1)} %param.14) | copy-start | bytes 393220
  6.5 31.9 %copy-start.4 = (bf16[128,512]{1,0:T(8,128)(2,1)S(1)}, bf16[128,512]{1,0:T(8,128)(2,1)}, u32[]{:S(2)}) copy-start(bf16[128,512]{1,0:T(8,128)(2,1)} %param.15) | copy-start | bytes 393220
  6.5 31.9 %copy-start.5 = (bf16[128,512]{1,0:T(8,128)(2,1)S(1)}, bf16[128,512]{1,0:T(8,128)(2,1)}, u32[]{:S(2)}) copy-start(bf16[128,512]{1,0:T(8,128)(2,1)} %param.13) | copy-start | bytes 393220
  6.5 98.2 %all-gather.3.cloned.1.call-start = ((), (), s32[]{:S(2)}) async-start(), calls=%async_computation.3 | async-start | bytes 7798784 | tf_op jit(solution)/shard_map/all_gather | solution.py:141
  7.3 215.2 %all-reduce.3.cloned.1.call-start = ((), (), s32[]{:S(2)}) async-start(), calls=%async_computation.6 | async-start | bytes 7340032
  8.4 71.6 %collective-permute-start.6 = (bf16[128,512]{0,1:T(8,128)(2,1)S(1)}, bf16[128,512]{0,1:T(8,128)(2,1)S(1)}, u32[]{:S(2)}, u32[]{:S(2)}) collective-permute-start(bf16[128,512]{0,1:T(8,128)(2,1)S(1)} %fusion.24), channel_id=1, source_target_pairs={{0,64},{16,80},{32,96},{48,112},{64,128},{80,144},{96,160},{112,17... | collective-permute-start | bytes 393224 | tf_op jit(solution)/shard_map/ppermute | solution.py:18
  13.6 66.5 %collective-permute-start.7 = (bf16[128,512]{0,1:T(8,128)(2,1)S(1)}, bf16[128,512]{0,1:T(8,128)(2,1)S(1)}, u32[]{:S(2)}, u32[]{:S(2)}) collective-permute-start(bf16[128,512]{0,1:T(8,128)(2,1)S(1)} %fusion.24), channel_id=1, source_target_pairs={{0,48},{16,64},{32,80},{48,96},{64,112},{80,128},{96,144},{112,160... | collective-permute-start | bytes 393224 | tf_op jit(solution)/shard_map/ppermute | solution.py:18
  17.8 81.6 %collective-permute-start.8 = (bf16[128,512]{0,1:T(8,128)(2,1)S(1)}, bf16[128,512]{0,1:T(8,128)(2,1)S(1)}, u32[]{:S(2)}, u32[]{:S(2)}) collective-permute-start(bf16[128,512]{0,1:T(8,128)(2,1)S(1)} %fusion.24), channel_id=1, source_target_pairs={{0,32},{16,48},{32,64},{48,80},{64,96},{80,112},{96,128},{112,144}... | collective-permute-start | bytes 393224 | tf_op jit(solution)/shard_map/ppermute | solution.py:18
  20.8 39.6 %collective-permute-start.2 = (bf16[128,512]{1,0:T(8,128)(2,1)}, bf16[128,512]{1,0:T(8,128)(2,1)S(1)}, u32[]{:S(2)}, u32[]{:S(2)}) collective-permute-start(bf16[128,512]{1,0:T(8,128)(2,1)} %param.15), channel_id=1, source_target_pairs={{0,64},{16,80},{32,96},{48,112},{64,128},{80,144},{96,160},{112,17... | collective-permute-start | bytes 393224 | tf_op jit(solution)/shard_map/ppermute | solution.py:18
  25.5 13.7 %collective-permute-start.1 = (bf16[16,512]{1,0:T(8,128)(2,1)}, bf16[16,512]{1,0:T(8,128)(2,1)S(1)}, u32[]{:S(2)}, u32[]{:S(2)}) collective-permute-start(bf16[16,512]{1,0:T(8,128)(2,1)} %slice.74), channel_id=1, source_target_pairs={{16,0},{32,16},{48,32},{64,48},{80,64},{96,80},{112,96},{128,112},... | collective-permute-start | bytes 49160 | tf_op jit(solution)/shard_map/ppermute | solution.py:18
  38.4 21.9 %copy-start.6 = (bf16[16,4,8,128]{3,2,1,0:T(8,128)(2,1)}, bf16[16,4,8,128]{3,2,1,0:T(8,128)(2,1)S(1)}, u32[]{:S(2)}) copy-start(bf16[16,4,8,128]{3,2,1,0:T(8,128)(2,1)S(1)} %fusion.25) | copy-start | bytes 393220
  39.1 24.5 %collective-permute-start.3 = (bf16[128,512]{1,0:T(8,128)(2,1)S(1)}, bf16[128,512]{1,0:T(8,128)(2,1)S(1)}, u32[]{:S(2)}, u32[]{:S(2)}) collective-permute-start(bf16[128,512]{1,0:T(8,128)(2,1)S(1)} %copy-done.4), channel_id=1, source_target_pairs={{0,48},{16,64},{32,80},{48,96},{64,112},{80,128},{96,144},{112,160... | collective-permute-start | bytes 393224 | tf_op jit(solution)/shard_map/ppermute | solution.py:18
  60.4 43.7 %copy-start.10 = (f32[128,4]{0,1:T(4,128)S(1)}, f32[128,4]{0,1:T(4,128)}, u32[]{:S(2)}) copy-start(f32[128,4]{0,1:T(4,128)} %get-tuple-element.8) | copy-start | bytes 6148
  60.4 10.8 %collective-permute-start.4 = (bf16[128,512]{1,0:T(8,128)(2,1)S(1)}, bf16[128,512]{1,0:T(8,128)(2,1)S(1)}, u32[]{:S(2)}, u32[]{:S(2)}) collective-permute-start(bf16[128,512]{1,0:T(8,128)(2,1)S(1)} %copy-done.4), channel_id=1, source_target_pairs={{0,32},{16,48},{32,64},{48,80},{64,96},{80,112},{96,128},{112,144}... | collective-permute-start | bytes 393224 | tf_op jit(solution)/shard_map/ppermute | solution.py:18
  63.6 10.6 %collective-permute-start.5 = (bf16[128,512]{1,0:T(8,128)(2,1)S(1)}, bf16[128,512]{1,0:T(8,128)(2,1)S(1)}, u32[]{:S(2)}, u32[]{:S(2)}) collective-permute-start(bf16[128,512]{1,0:T(8,128)(2,1)S(1)} %copy-done.4), channel_id=1, source_target_pairs={{0,16},{16,32},{32,48},{48,64},{64,80},{80,96},{96,112},{112,128},... | collective-permute-start | bytes 393224 | tf_op jit(solution)/shard_map/ppermute | solution.py:18
  71.2 29.0 %collective-permute-start.9 = (bf16[128,512]{0,1:T(8,128)(2,1)S(1)}, bf16[128,512]{0,1:T(8,128)(2,1)}, u32[]{:S(2)}, u32[]{:S(2)}) collective-permute-start(bf16[128,512]{0,1:T(8,128)(2,1)S(1)} %fusion.24), channel_id=1, source_target_pairs={{0,16},{16,32},{32,48},{48,64},{64,80},{80,96},{96,112},{112,128},... | collective-permute-start | bytes 393224 | tf_op jit(solution)/shard_map/ppermute | solution.py:18
  74.2 4.2 %collective-permute-start = (bf16[16,512]{1,0:T(8,128)(2,1)}, bf16[16,512]{1,0:T(8,128)(2,1)S(1)}, u32[]{:S(2)}, u32[]{:S(2)}) collective-permute-start(bf16[16,512]{1,0:T(8,128)(2,1)} %slice.66), channel_id=1, source_target_pairs={{16,0},{32,16},{48,32},{64,48},{80,64},{96,80},{112,96},{128,112},... | collective-permute-start | bytes 49160 | tf_op jit(solution)/shard_map/ppermute | solution.py:18
  80.1 24.4 %copy-start.9 = (f32[128,4]{0,1:T(4,128)S(1)}, f32[128,4]{0,1:T(4,128)}, u32[]{:S(2)}) copy-start(f32[128,4]{0,1:T(4,128)} %get-tuple-element.7) | copy-start | bytes 6148
  80.2 18.8 %copy-start.8 = (bf16[640,512]{0,1:T(8,128)(2,1)}, bf16[640,512]{0,1:T(8,128)(2,1)S(1)}, u32[]{:S(2)}) copy-start(bf16[640,512]{0,1:T(8,128)(2,1)S(1)} %constant_dynamic-update-slice_fusion.8) | copy-start | bytes 1966084
  99.3 5.2 %copy-start.15 = (bf16[4,128,128]{1,2,0:T(8,128)(2,1)S(1)}, bf16[4,128,128]{1,2,0:T(8,128)(2,1)}, u32[]{:S(2)}) copy-start(bf16[4,128,128]{1,2,0:T(8,128)(2,1)} %get-tuple-element.16) | copy-start | bytes 393220
  112.2 0.7 copy-start.11
  112.2 1.3 copy-start.14
  112.2 110.2 %copy-start.3 = (bf16[8,7168]{1,0:T(8,128)(2,1)S(1)}, bf16[8,7168]{1,0:T(8,128)(2,1)}, u32[]{:S(2)}) copy-start(bf16[8,7168]{1,0:T(8,128)(2,1)} %param.19) | copy-start | bytes 344068
  112.2 111.4 %copy-start.7 = (f32[7168]{0:T(1024)S(1)}, f32[7168]{0:T(1024)}, u32[]{:S(2)}) copy-start(f32[7168]{0:T(1024)} %param.20) | copy-start | bytes 86020
  112.3 175.7 %all-gather.5.cloned.1.call-start = ((), (), s32[]{:S(2)}) async-start(), calls=%async_computation.4 | async-start | bytes 7798784 | tf_op jit(solution)/shard_map/all_gather | solution.py:170
  240.5 142.0 %reduce-scatter.2.cloned.1.call-start = ((), (), s32[]{:S(2)}) async-start(), calls=%async_computation.5 | async-start | bytes 7798784 | tf_op jit(solution)/shard_map/reduce_scatter | solution.py:178
  303.4 5.8 %copy-start.1 = (bf16[512,7168]{1,0:T(8,128)(2,1)S(1)}, bf16[512,7168]{1,0:T(8,128)(2,1)}, u32[]{:S(2)}) copy-start(bf16[512,7168]{1,0:T(8,128)(2,1)} %reshape.232) | copy-start | bytes 22020100
  303.4 6.2 %copy-start.13 = (bf16[1,7168,128]{2,1,0:T(8,128)(2,1)S(1)}, bf16[1,7168,128]{2,1,0:T(8,128)(2,1)}, u32[]{:S(2)}) copy-start(bf16[1,7168,128]{2,1,0:T(8,128)(2,1)} %param.24) | copy-start | bytes 5505028
  316.7 74.9 %copy-start.12 = (f32[8,2]{0,1:T(2,128)S(1)}, f32[8,2]{0,1:T(2,128)}, u32[]{:S(2)}) copy-start(f32[8,2]{0,1:T(2,128)} %param.22) | copy-start | bytes 196
  384.8 16.8 %all-to-all-start.1 = ((bf16[16,2,7168]{2,1,0:T(2,128)(2,1)}), bf16[16,2,7168]{2,1,0:T(2,128)(2,1)S(1)}, u32[]{:S(2)}, u32[]{:S(2)}) async-start(bf16[16,2,7168]{2,1,0:T(2,128)(2,1)} %copy.99), calls=%async_computation.2 | async-start | bytes 917504 | tf_op jit(solution)/shard_map/all_to_all | solution.py:181
Sparse Core Ops, SparseCore 0:
  9.2 66.9 all-gather.2
  112.4 110.0 all-reduce.2
  240.6 47.3 all-gather.4
  316.8 65.6 reduce-scatter.1
where the time goes:
time: 414 us; the launch traced here: 410 us
  waiting for transfers between devices  240 us (58%)
  blocking collectives  52.5 us (13%)
  starting transfers between devices  37.3 us (9%)
  local copies, waits for them, and re-layouts  31.5 us (8%)
  matrix products  29.6 us (7%)
  between operations  14.3 us (3%)
  other arithmetic  5.37 us (1%)
    unnamed x5, waiting for transfers between devices  108 us
    reduce_scatter x1, waiting for transfers between devices, local(): lax.psum_scatter(partial_out.astype(jnp.bfloat16), 'ctx', scatter_dimensi...  65.8 us
    all_gather x1, waiting for transfers between devices, local(): portion = lax.all_gather(arrived, 'ctx', axis=0, tiled=True)  47.3 us
    ppermute x10, starting transfers between devices, passed_along(): return lax.ppermute(block, axis, route)  30.1 us
    all_gather x1, blocking collectives, local(): part_values = lax.all_gather(comp_values, 'ctx', axis=0, tiled=True)  18.8 us
    all_gather x1, blocking collectives, local(): part_keys = lax.all_gather(comp_keys, 'ctx', axis=0, tiled=True)  18.3 us
    reshape x1, local copies, waits for them, and re-layouts, local(): flat_rows = portion.reshape(-1, model_width)  15.4 us
    all_to_all x1, blocking collectives, local(): lax.all_to_all(outgoing, 'exp', split_axis=0, concat_axis=0, tiled=True)  15.4 us
  transfers between devices with their start and end apart: 15, of which 7 were waited for; matrix products, arithmetic and copies ran while one was open for 6% of the time, Pallas kernels for 0%

commit v1 on v0

v1 whole, which is shorter than its diff:
```python
import math

import jax
import jax.numpy as jnp
from jax import lax
from jax.experimental import pallas as pl
from jax.experimental.pallas import tpu as pltpu
from jax.sharding import PartitionSpec as P

MESH = pl.DeviceIdType.MESH
BF = jnp.bfloat16
F32 = jnp.float32
WINDOW = 512
SCALE = 2.0 / math.sqrt(128)
EPS = 1e-06


def place():
    c = lax.axis_index("ctx")
    e = lax.axis_index("exp")
    return lax.div(c, 2), lax.rem(c, 2), e


def greet(devices):
    bar = pltpu.get_barrier_semaphore()
    for d in devices:
        pl.semaphore_signal(bar, inc=1, device_id=d, device_id_type=MESH)
    pl.semaphore_wait(bar, len(devices))


def rcopy(src, dst, ss, rs, dev):
    return pltpu.make_async_remote_copy(
        src_ref=src, dst_ref=dst, send_sem=ss, recv_sem=rs, device_id=dev, device_id_type=MESH
    )


def unit(x):
    return x * lax.rsqrt(jnp.mean(x * x, axis=1, keepdims=True) + EPS)


def attention(
    q, k, v, g, cw, wo, eg, eu, ed,
    att, wpair, sg, su, sd,
    kb, vb, qb, gb, hk, hv, cb, tb, ss, rs,
):
    z, core, e = place()
    other = 1 - core
    up, down = lax.rem(z + 1, 8), lax.rem(z + 7, 8)
    sib = (2 * z + other, e)
    peers = [(2 * lax.rem(z + j, 8) + core, e) for j in range(1, 8)]
    greet([sib, (2 * up + other, e), (2 * down + other, e)] + peers)

    off_other = pl.multiple_of(other * 256, 256)
    off = pl.multiple_of(core * 256, 256)
    near = []
    for kk in range(2):
        for a, (src, dst) in enumerate(((k, kb), (v, vb))):
            near.append(
                rcopy(
                    src.at[:, pl.ds(kk * 256, 256)],
                    dst.at[1, core],
                    ss.at[8 + 2 * kk + a],
                    rs.at[8 + 2 * core + a],
                    (2 * up + kk, e),
                )
            )
    halo = []
    for kk in range(2):
        for a, (src, dst) in enumerate(((k, hk), (v, hv))):
            halo.append(
                rcopy(
                    src.at[pl.ds(0, 16), pl.ds(kk * 256, 256)],
                    dst,
                    ss.at[16 + 2 * kk + a],
                    rs.at[16 + a],
                    (2 * down + kk, e),
                )
            )

    @pl.when(core == 0)
    def _():
        for cp in halo:
            cp.start()

    swap = [
        rcopy(k.at[:, pl.ds(off_other, 256)], kb.at[2, core], ss.at[0], rs.at[0], sib),
        rcopy(v.at[:, pl.ds(off_other, 256)], vb.at[2, core], ss.at[1], rs.at[1], sib),
        rcopy(q.at[:, pl.ds(off_other, 256)], qb.at[core], ss.at[2], rs.at[2], sib),
        rcopy(g, gb.at[core], ss.at[3], rs.at[3], sib),
    ]
    for cp in swap:
        cp.start()
    for cp in near:
        cp.start()
    share = [
        rcopy(wo, wpair.at[core], ss.at[4], rs.at[4], sib),
        rcopy(eg, sg, ss.at[5], rs.at[5], sib),
        rcopy(eu, su, ss.at[6], rs.at[6], sib),
        rcopy(ed, sd, ss.at[7], rs.at[7], sib),
    ]
    for cp in share:
        cp.start()

    kb[2, core] = k[:, pl.ds(off, 256)]
    vb[2, core] = v[:, pl.ds(off, 256)]
    qb[core] = q[:, pl.ds(off, 256)]
    gb[core] = g[...]
    wpair[core] = wo[...]

    for cp in swap:
        cp.wait_recv()
    halo[0].wait_recv()
    halo[1].wait_recv()

    for a, (blocks, tail) in enumerate(((kb, hk), (vb, hv))):
        for h in range(2):
            hs = h * 128
            last = jnp.where(z == 7, 0.0, tail[:, hs : hs + 128].astype(F32))
            x = jnp.concatenate(
                [
                    blocks[2, 0, :, hs : hs + 128].astype(F32),
                    blocks[2, 1, :, hs : hs + 128].astype(F32),
                    last,
                ],
                0,
            ).reshape(17, 16, 128)
            w = cw[a, 2 * core + h]
            y = jnp.sum(x[:16] * w[None, :16], axis=1) + jnp.sum(x[1:] * w[None, 16:], axis=1)
            if a == 0:
                y = unit(y)
            cb[z, a, :, hs : hs + 128] = y.astype(BF)
    comps = [
        rcopy(cb.at[z], cb.at[z], ss.at[20 + j], rs.at[20 + j], peers[j - 1]) for j in range(1, 8)
    ]
    for cp in comps:
        cp.start()

    relay = []
    for s in range(2):
        for a, buf in enumerate((kb, vb)):
            rcopy(buf.at[1, s], buf.at[1, s], ss.at[8], rs.at[8 + 2 * s + a], sib).wait_recv()
            cp = rcopy(
                buf.at[1, s],
                buf.at[0, s],
                ss.at[12 + 2 * s + a],
                rs.at[12 + 2 * s + a],
                (2 * up + core, e),
            )
            cp.start()
            relay.append(cp)
    for cp in comps:
        cp.wait_recv()
    for cp in relay:
        cp.wait_recv()

    pos = z * 256 + lax.broadcasted_iota(jnp.int32, (256, 1), 0)
    block_end = lax.broadcasted_iota(jnp.int32, (1, 128), 1) * 16 + 31
    key_pos = (z - 2) * 256 + lax.broadcasted_iota(jnp.int32, (1, 768), 1)
    lane = lax.broadcasted_iota(jnp.int32, (1, 128), 1)
    gates = gb[...].reshape(256, 128)
    gates = 1.0 / (1.0 + jnp.exp(-gates))
    for h in range(2):
        hs = h * 128
        qn = unit(qb[:, :, hs : hs + 128].reshape(256, 128).astype(F32)).astype(BF)
        ck = cb[:, 0, :, hs : hs + 128].reshape(128, 128)
        cv = cb[:, 1, :, hs : hs + 128].reshape(128, 128)
        s1 = lax.dot_general(qn, ck, (((1,), (1,)), ((), ())), preferred_element_type=F32)
        w1 = jnp.where(block_end <= pos, jnp.exp(SCALE * s1), 0.0)
        t1 = jnp.sum(w1, axis=1, keepdims=True) + (pos < 31).astype(F32)
        o1 = jnp.dot(w1.astype(BF), cv, preferred_element_type=F32) / t1
        kn = unit(kb[:, :, :, hs : hs + 128].reshape(768, 128).astype(F32)).astype(BF)
        vn = vb[:, :, :, hs : hs + 128].reshape(768, 128)
        s2 = lax.dot_general(qn, kn, (((1,), (1,)), ((), ())), preferred_element_type=F32)
        inside = (key_pos <= pos) & (key_pos > pos - WINDOW) & (key_pos >= 0)
        w2 = jnp.where(inside, jnp.exp(SCALE * s2), 0.0)
        t2 = jnp.sum(w2, axis=1, keepdims=True)
        o2 = jnp.dot(w2.astype(BF), vn, preferred_element_type=F32) / t2
        g1 = jnp.sum(jnp.where(lane == 2 * core + h, gates, 0.0), axis=1, keepdims=True)
        g2 = jnp.sum(jnp.where(lane == 4 + 2 * core + h, gates, 0.0), axis=1, keepdims=True)
        tb[:, :, hs : hs + 128] = (g1 * o1 + g2 * o2).astype(BF).reshape(2, 128, 128)
    back = rcopy(tb.at[other], att.at[core], ss.at[28], rs.at[28], sib)
    back.start()
    att[core] = tb[core]

    @pl.when(core == 0)
    def _():
        for cp in halo:
            cp.wait_send()

    for cp in swap + near + comps + relay:
        cp.wait_send()
    for cp in share + [back]:
        cp.wait()


def run_attention(q, k, v, g, cw, wo, eg, eu, ed):
    vm = pl.BlockSpec(memory_space=pltpu.VMEM)
    hbm = pl.BlockSpec(memory_space=pl.ANY)
    return pl.pallas_call(
        attention,
        out_shape=(
            jax.ShapeDtypeStruct((2, 128, 256), BF),
            jax.ShapeDtypeStruct((2, 512, 448), BF),
            jax.ShapeDtypeStruct(eg.shape, BF),
            jax.ShapeDtypeStruct(eu.shape, BF),
            jax.ShapeDtypeStruct(ed.shape, BF),
        ),
        in_specs=[vm] * 6 + [hbm] * 3,
        out_specs=(vm, vm, hbm, hbm, hbm),
        scratch_shapes=[
            pltpu.VMEM((3, 2, 128, 256), BF),
            pltpu.VMEM((3, 2, 128, 256), BF),
            pltpu.VMEM((2, 128, 256), BF),
            pltpu.VMEM((2, 128, 128), F32),
            pltpu.VMEM((16, 256), BF),
            pltpu.VMEM((16, 256), BF),
            pltpu.VMEM((8, 2, 16, 256), BF),
            pltpu.VMEM((2, 128, 256), BF),
            pltpu.SemaphoreType.DMA((29,)),
            pltpu.SemaphoreType.DMA((29,)),
        ],
        compiler_params=pltpu.CompilerParams(
            collective_id=1, has_side_effects=True, vmem_limit_bytes=32 << 20
        ),
        name="attention",
    )(q, k, v, g, cw, wo, eg, eu, ed)


def z_ring(buf, z, core, e, ss, rs):
    up, down = lax.rem(z + 1, 8), lax.rem(z + 7, 8)

    def copy(way, step, chunk):
        block = lax.rem(z + 8 - step, 8) if way == 0 else lax.rem(z + step, 8)
        slot = way * 7 + 2 * step + (chunk if step < 3 else 0)
        return rcopy(
            buf.at[block, chunk],
            buf.at[block, chunk],
            ss.at[slot],
            rs.at[slot],
            (2 * (up if way == 0 else down) + core, e),
        )

    def chunks(way, step):
        return (0, 1) if step < 3 else ((0,) if way == 0 else (1,))

    return copy, chunks


def gather_start(copy, chunks, sent):
    for chunk in (0, 1):
        for way in (0, 1):
            cp = copy(way, 0, chunk)
            cp.start()
            sent.append(cp)


def gather_step(copy, chunks, step, sent):
    for chunk in (0, 1):
        for way in (0, 1):
            if chunk in chunks(way, step):
                copy(way, step, chunk).wait_recv()
                if step < 3 and chunk in chunks(way, step + 1):
                    cp = copy(way, step + 1, chunk)
                    cp.start()
                    sent.append(cp)


def project(
    att, wp,
    hid,
    xb, pb, a1, a2, a3, sb, c1, c2, c3, rb, ss, rs, s1, r1, s2, r2, s3, r3,
):
    z, core, e = place()
    ex, ey = lax.div(e, 4), lax.rem(e, 4)
    c = 2 * z + core
    ring = [
        (ex, lambda t: (c, 4 * lax.rem(t, 4) + ey)),
        (ey, lambda t: (c, 4 * ex + lax.rem(t, 4))),
    ]
    zp = [(2 * lax.rem(z + j, 8) + core, e) for j in range(1, 8)]
    greet([dev(p + j) for p, dev in ring for j in (1, 3)] + zp)

    xb[z] = att[...]
    copy, chunks = z_ring(xb, z, core, e, ss, rs)
    sent = []
    gather_start(copy, chunks, sent)

    def partial(block, r):
        x0, x1 = xb[block, 0], xb[block, 1]
        parts = [
            jnp.dot(x0, wp[n, :256], preferred_element_type=F32)
            + jnp.dot(x1, wp[n, 256:], preferred_element_type=F32)
            for n in range(2)
        ]
        pb[r] = jnp.concatenate(parts, 1).reshape(4, 4, 8, 896).astype(BF)

    partial(z, 0)
    for step in range(4):
        gather_step(copy, chunks, step, sent)
        partial(lax.rem(z + step + 1, 8), step + 1)
        if step < 3:
            partial(lax.rem(z + 7 - step, 8), 7 - step)

    def ring_sum(which, half, piece, first, second, mixed, ssem, rsem):
        p, dev = ring[which]
        nxt, prv = dev(p + 1), dev(p + 3)
        base = 6 * half
        far, nt, pt = lax.rem(p + 2, 4), lax.rem(p + 1, 4), lax.rem(p + 3, 4)
        cps = [
            rcopy(piece(far, 0), first.at[half, 0], ssem.at[base], rsem.at[base], nxt),
            rcopy(piece(far, 1), first.at[half, 1], ssem.at[base + 1], rsem.at[base + 1], prv),
            rcopy(piece(nt, 1), second.at[half, 0, pl.ds(2, 2)], ssem.at[base + 2], rsem.at[base + 2], nxt),
            rcopy(piece(pt, 0), second.at[half, 1, pl.ds(0, 2)], ssem.at[base + 3], rsem.at[base + 3], prv),
            rcopy(mixed.at[half, 0], second.at[half, 0, pl.ds(0, 2)], ssem.at[base + 4], rsem.at[base + 4], nxt),
            rcopy(mixed.at[half, 1], second.at[half, 1, pl.ds(2, 2)], ssem.at[base + 5], rsem.at[base + 5], prv),
        ]

        def start():
            for cp in cps[:4]:
                cp.start()

        def middle():
            cps[0].wait_recv()
            mixed[half, 0] = (first[half, 0].astype(F32) + piece(nt, 0)[...].astype(F32)).astype(BF)
            cps[4].start()
            cps[1].wait_recv()
            mixed[half, 1] = (first[half, 1].astype(F32) + piece(pt, 1)[...].astype(F32)).astype(BF)
            cps[5].start()

        def end():
            for cp in cps[2:]:
                cp.wait_recv()
            return [
                piece(p, n)[...].astype(F32)
                + second[half, 0, 2 * n : 2 * n + 2].astype(F32)
                + second[half, 1, 2 * n : 2 * n + 2].astype(F32)
                for n in range(2)
            ]

        def drain():
            for cp in cps:
                cp.wait_send()

        return start, middle, end, drain

    def piece_a(t, n):
        return pb.at[pl.ds(2 * n, 2), t]

    def piece_b(t, n):
        return pb.at[pl.ds(4 + 2 * n, 2), :, t]

    def piece_of(half):
        return lambda t, n: sb.at[half, pl.ds(2 * n, 2), t]

    wide = [
        ring_sum(0, 0, piece_a, a1, a2, a3, s1, r1),
        ring_sum(1, 1, piece_b, a1, a2, a3, s1, r1),
    ]
    thin = [
        ring_sum(1, 0, piece_of(0), c1, c2, c3, s2, r2),
        ring_sum(0, 1, piece_of(1), c1, c2, c3, s2, r2),
    ]
    for r in wide:
        r[0]()
    for r in wide:
        r[1]()
    for half in range(2):
        lo, hi = wide[half][2]()
        sb[half, 0:2] = lo.astype(BF)
        sb[half, 2:4] = hi.astype(BF)
        thin[half][0]()
    for r in thin:
        r[1]()
    out = []
    for half in range(2):
        lo, hi = thin[half][2]()
        rb[4 * half : 4 * half + 2] = lo.astype(BF)
        rb[4 * half + 2 : 4 * half + 4] = hi.astype(BF)
        for j in range(4 * half, 4 * half + 4):
            if j:
                cp = rcopy(rb.at[j], hid.at[z], s3.at[j], r3.at[j], zp[j - 1])
                cp.start()
                out.append(cp)
    hid[z] = rb[0]
    for cp in out:
        cp.wait()
    for cp in sent:
        cp.wait_send()
    for r in wide + thin:
        r[3]()


def run_project(att, wp):
    vm = pl.BlockSpec(memory_space=pltpu.VMEM)
    return pl.pallas_call(
        project,
        out_shape=jax.ShapeDtypeStruct((8, 8, 896), BF),
        in_specs=[vm] * 2,
        out_specs=vm,
        scratch_shapes=[
            pltpu.VMEM((8, 2, 128, 256), BF),
            pltpu.VMEM((8, 4, 4, 8, 896), BF),
            pltpu.VMEM((2, 2, 2, 4, 8, 896), BF),
            pltpu.VMEM((2, 2, 4, 4, 8, 896), BF),
            pltpu.VMEM((2, 2, 2, 4, 8, 896), BF),
            pltpu.VMEM((2, 4, 4, 8, 896), BF),
            pltpu.VMEM((2, 2, 2, 8, 896), BF),
            pltpu.VMEM((2, 2, 4, 8, 896), BF),
            pltpu.VMEM((2, 2, 2, 8, 896), BF),
            pltpu.VMEM((8, 8, 896), BF),
            pltpu.SemaphoreType.DMA((14,)),
            pltpu.SemaphoreType.DMA((14,)),
            pltpu.SemaphoreType.DMA((12,)),
            pltpu.SemaphoreType.DMA((12,)),
            pltpu.SemaphoreType.DMA((12,)),
            pltpu.SemaphoreType.DMA((12,)),
            pltpu.SemaphoreType.DMA((8,)),
            pltpu.SemaphoreType.DMA((8,)),
        ],
        compiler_params=pltpu.CompilerParams(
            collective_id=2, has_side_effects=True, vmem_limit_bytes=40 << 20
        ),
        name="project",
    )(att, wp)


def experts(
    outg, eg, eu, ed, sg, su, sd,
    ret,
    gw, dw, arr, xb, ob, rv, mx, fs, ro, ls, s0, r0, ss, rs, s1, r1, s2, r2,
):
    z, core, e = place()
    c = 2 * z + core
    up, down = (2 * lax.rem(z + 1, 8) + core, e), (2 * lax.rem(z + 7, 8) + core, e)
    plane = [(c, lax.rem(e + j, 16)) for j in range(1, 16)]
    greet(plane + [up, down])

    go = []
    for j in range(1, 16):
        cp = rcopy(outg.at[lax.rem(e + j, 16)], arr.at[e], s0.at[j], r0.at[j], plane[j - 1])
        cp.start()
        go.append(cp)
    load = [
        pltpu.make_async_copy(src, gw.at[:, pl.ds(128 * n, 128)], ls.at[n])
        for n, src in enumerate((eg, sg, eu, su))
    ] + [
        pltpu.make_async_copy(src, dw.at[pl.ds(128 * n, 128), :], ls.at[4 + n])
        for n, src in enumerate((ed, sd))
    ]
    for cp in load:
        cp.start()
    arr[e] = outg[e]
    for cp in go:
        cp.wait_recv()
    for i in range(16):
        fs[2 * i : 2 * i + 2, :] = arr[i].astype(F32)
    xb[z, 0] = fs[0:16].astype(BF)
    xb[z, 1] = fs[16:32].astype(BF)

    copy, chunks = z_ring(xb, z, core, e, ss, rs)
    sent = []
    gather_start(copy, chunks, sent)
    for cp in load:
        cp.wait()

    def work(a, b):
        x = jnp.concatenate([xb[a, 0], xb[a, 1], xb[b, 0], xb[b, 1]], 0)
        y = jnp.dot(x, gw[...], preferred_element_type=F32)
        gate, lift = y[:, :256], y[:, 256:]
        act = (gate / (1.0 + jnp.exp(-gate)) * lift).astype(BF)

        @pl.loop(0, 7)
        def _(n):
            cols = pl.ds(pl.multiple_of(n * 1024, 1024), 1024)
            out = jnp.dot(act, dw[:, cols], preferred_element_type=F32).astype(BF)
            ob[a, 0, :, cols] = out[0:16]
            ob[a, 1, :, cols] = out[16:32]
            ob[b, 0, :, cols] = out[32:48]
            ob[b, 1, :, cols] = out[48:64]

    for step in range(4):
        gather_step(copy, chunks, step, sent)
        if step < 3:
            work(lax.rem(z + step + 1, 8), lax.rem(z + 7 - step, 8))
        else:
            work(lax.rem(z + 4, 8), z)

    def leg(way, slot, src):
        return rcopy(
            src, rv.at[way, slot], s1.at[way * 7 + slot], r1.at[way * 7 + slot], up if way == 0 else down
        )

    def mine(way, dist, first):
        block = lax.rem(z + dist, 8) if way == 0 else lax.rem(z + 8 - dist, 8)
        chunk = first if way == 0 else 1 - first
        return ob.at[block, chunk]

    back = []

    def send(way, slot, src):
        cp = leg(way, slot, src)
        cp.start()
        back.append(cp)

    for way in (0, 1):
        send(way, 0, mine(way, 4, 0))
    for way in (0, 1):
        send(way, 2, mine(way, 3, 1))
    for slot, dist, first, source in ((1, 3, 0, 0), (3, 2, 0, 1), (4, 2, 1, 2), (5, 1, 0, 3), (6, 1, 1, 4)):
        for way in (0, 1):
            leg(way, source, rv.at[way, source]).wait_recv()
            mx[way, slot] = (
                rv[way, source].astype(F32) + mine(way, dist, first)[...].astype(F32)
            ).astype(BF)
            send(way, slot, mx.at[way, slot])
    for chunk in range(2):
        total = ob[z, chunk].astype(F32)
        for way in (0, 1):
            slot = 5 + (chunk if way == 0 else 1 - chunk)
            leg(way, slot, rv.at[way, slot]).wait_recv()
            total = total + rv[way, slot].astype(F32)
        fs[16 * chunk : 16 * chunk + 16] = total
    for i in range(16):
        ro[i] = fs[2 * i : 2 * i + 2, :].astype(BF)
    home = []
    for j in range(1, 16):
        cp = rcopy(ro.at[lax.rem(e + j, 16)], ret.at[e], s2.at[j], r2.at[j], plane[j - 1])
        cp.start()
        home.append(cp)
    ret[e] = ro[e]
    for cp in home:
        cp.wait()
    for cp in go + sent + back:
        cp.wait_send()


def run_experts(outg, eg, eu, ed, sg, su, sd):
    vm = pl.BlockSpec(memory_space=pltpu.VMEM)
    hbm = pl.BlockSpec(memory_space=pl.ANY)
    return pl.pallas_call(
        experts,
        out_shape=jax.ShapeDtypeStruct((16, 2, 7168), BF),
        in_specs=[vm] + [hbm] * 6,
        out_specs=vm,
        scratch_shapes=[
            pltpu.VMEM((7168, 512), BF),
            pltpu.VMEM((256, 7168), BF),
            pltpu.VMEM((16, 2, 7168), BF),
            pltpu.VMEM((8, 2, 16, 7168), BF),
            pltpu.VMEM((8, 2, 16, 7168), BF),
            pltpu.VMEM((2, 7, 16, 7168), BF),
            pltpu.VMEM((2, 7, 16, 7168), BF),
            pltpu.VMEM((32, 7168), F32),
            pltpu.VMEM((16, 2, 7168), BF),
            pltpu.SemaphoreType.DMA((6,)),
            pltpu.SemaphoreType.DMA((16,)),
            pltpu.SemaphoreType.DMA((16,)),
            pltpu.SemaphoreType.DMA((14,)),
            pltpu.SemaphoreType.DMA((14,)),
            pltpu.SemaphoreType.DMA((14,)),
            pltpu.SemaphoreType.DMA((14,)),
            pltpu.SemaphoreType.DMA((16,)),
            pltpu.SemaphoreType.DMA((16,)),
        ],
        compiler_params=pltpu.CompilerParams(
            collective_id=3, has_side_effects=True, vmem_limit_bytes=58 << 20
        ),
        name="experts",
    )(outg, eg, eu, ed, sg, su, sd)


def local(
    query_input,
    key_input,
    value_input,
    gate_logits,
    comp_weight,
    out_proj,
    residual_in,
    ffn_gain,
    expert_ids,
    route_gates,
    expert_gate,
    expert_up,
    expert_down,
):
    gates = jnp.pad(gate_logits.transpose(1, 0, 2).reshape(128, 8), ((0, 0), (0, 120)))
    cw = jnp.broadcast_to(comp_weight.transpose(0, 2, 1)[..., None], (2, 4, 32, 128))
    att, wpair, sg, su, sd = run_attention(
        query_input, key_input, value_input, gates, cw, out_proj,
        expert_gate[0], expert_up[0], expert_down[0],
    )
    projected = run_project(att, wpair)
    projected = projected.transpose(1, 0, 2).reshape(8, 7168).astype(F32)
    hidden_state = residual_in.astype(F32) + projected
    mean_square = jnp.mean(hidden_state * hidden_state, axis=1, keepdims=True)
    normed = (hidden_state * lax.rsqrt(mean_square + EPS) * ffn_gain).astype(BF)

    flat_ids = expert_ids.reshape(-1)
    chosen = (flat_ids[:, None] == jnp.arange(16, dtype=jnp.int32)[None, :]).astype(jnp.int32)
    slots = jnp.sum((jnp.cumsum(chosen, axis=0) - chosen) * chosen, axis=1)
    targets = (flat_ids * 2 + slots).reshape(8, 2)
    slot_range = jnp.arange(32, dtype=jnp.int32)
    dispatch_map = jnp.sum(
        (slot_range[:, None, None] == targets[None, :, :]).astype(F32), axis=2
    ).astype(BF)
    outgoing = (
        jnp.dot(dispatch_map, normed, preferred_element_type=F32).astype(BF).reshape(16, 2, 7168)
    )
    returned = run_experts(
        outgoing, expert_gate[0], expert_up[0], expert_down[0], sg, su, sd
    ).reshape(32, 7168)
    combine_map = jnp.sum(
        jnp.where(slot_range[None, None, :] == targets[:, :, None], route_gates[:, :, None], 0.0),
        axis=1,
    )
    moe_out = jnp.dot(combine_map, returned.astype(F32), precision=lax.Precision.HIGHEST)
    return (hidden_state + moe_out).astype(BF)


def solution(mesh):
    in_specs = (
        P("ctx", "exp"),
        P("ctx", "exp"),
        P("ctx", "exp"),
        P(None, "ctx", "exp"),
        P(None, None, "exp"),
        P("exp", "ctx"),
        P(("ctx", "exp"), None),
        P(),
        P(("ctx", "exp"), None),
        P(("ctx", "exp"), None),
        P("exp", None, "ctx"),
        P("exp", None, "ctx"),
        P("exp", "ctx", None),
    )
    out_specs = P(("ctx", "exp"), None)
    return jax.shard_map(local, mesh=mesh, in_specs=in_specs, out_specs=out_specs, check_vma=False)
```

time: 414 us -> 178 us (0.43)
  waiting for transfers between devices: 240 us -> 0 us
  Pallas kernels: 0 us -> 158 us
  blocking collectives: 52.5 us -> 0 us
  starting transfers between devices: 37.3 us -> 0 us
  matrix products: 29.6 us -> 1.29 us
  local copies, waits for them, and re-layouts: 31.5 us -> 16.2 us
  between operations: 14.3 us -> 0.12 us
  other arithmetic: 5.37 us -> 0.66 us
    pallas_call x0 -> x3, Pallas kernels: none -> 158 us  [the longest x1 88.8 us: run_experts(): pl.pallas_call(experts, out_shape=jax.ShapeDtypeStruct((16, 2, 7168), BF)...]
    unnamed x5 -> x0, waiting for transfers between devices: 108 us -> none
    reduce_scatter x1 -> x0, waiting for transfers between devices: 65.8 us -> none  [local(): lax.psum_scatter(partial_out.astype(jnp.bfloat16), 'ctx', scatter_dimensi...]
    all_gather x2 -> x0, waiting for transfers between devices: 47.3 us -> none  [the longest x1 47.3 us: local(): portion = lax.all_gather(arrived, 'ctx', axis=0, tiled=True)]
    all_gather x2 -> x0, blocking collectives: 37.2 us -> none  [the longest x1 18.8 us: local(): part_values = lax.all_gather(comp_values, 'ctx', axis=0, tiled=True)]
    ppermute x10 -> x0, starting transfers between devices: 30.1 us -> none  [passed_along(): return lax.ppermute(block, axis, route)]
    dot_general x14 -> x2, matrix products: 29.6 us -> 1.29 us  [the longest x1 0.95 us: local(): jnp.dot(combine_map, returned.astype(F32), precision=lax.Precision.HIGHEST)]
    all_to_all x1 -> x0, blocking collectives: 15.4 us -> none  [local(): lax.all_to_all(outgoing, 'exp', split_axis=0, concat_axis=0, tiled=True)]
  transfers between devices with their start and end apart: 15 -> 0, of which waited for: 7 -> 0; matrix products, arithmetic and copies ran while one was open for 6% -> 0% of each run, Pallas kernels for 0% -> 0%
where the time goes in v1:
time: 178 us; the launch traced here: 176 us
  Pallas kernels  158 us (89%)
  local copies, waits for them, and re-layouts  16.2 us (9%)
    pallas_call x1, Pallas kernels, run_experts(): pl.pallas_call(experts, out_shape=jax.ShapeDtypeStruct((16, 2, 7168), BF)...  88.8 us
    pallas_call x1, Pallas kernels, run_project(): pl.pallas_call(project, out_shape=jax.ShapeDtypeStruct((8, 8, 896), BF),...  45 us
    pallas_call x1, Pallas kernels, run_attention(): pl.pallas_call(attention, out_shape=(jax.ShapeDtypeStruct((2, 128, 256),...  24.4 us
    unnamed x28, local copies, waits for them, and re-layouts  12.2 us

profile of v1, /device:TPU:32, one launch (start us, length us, event | category | flops | bytes accessed | tf_op | source)
XLA Modules:
  0.0 176.5 jit_solution(154466045575334301)
XLA Ops:
  0.0 1.2 copy.25.wo
  1.2 0.8 broadcast_in_dim.10.cw
  2.0 0.8 copy.24
  2.8 0.0 copy-start
  2.8 1.5 copy-done
  4.3 1.5 copy-done.1
  5.8 1.5 copy-done.2
  7.3 0.9 copy-done.6
  8.2 0.9 copy-done.7
  9.1 0.9 copy-done.8
  10.0 24.4 %attention.1 = (bf16[2,128,256]{2,1,0:T(8,128)(2,1)S(1)}, bf16[2,512,448]{2,1,0:T(8,128)(2,1)S(1)}, bf16[7168,128]{1,0:T(8,128)(2,1)S(1)}, bf16[7168,128]{1,0:T(8,128)(2,1)S(1)}, bf16[128,7168]{1,0:T(8,128)(2,1)S(1)}) custom-call(bf16[128,512]{1,0:T(8,128)(2,1)S(1)} %copy-done.6, bf16[128,512]{1,0:T(8,128)(2,1)S(1)} %copy-done.7, ...), custom_call_target="tpu_custom_call" | custom-call | tf_op jit(solution)/shard_map/attention/pallas_call | solution.py:199
  34.4 0.0 copy-start.3
  34.4 1.2 copy-done.3
  35.7 1.2 copy-done.4
  36.9 1.2 copy-done.5
  38.1 45.0 %project.1 = bf16[8,8,896]{2,1,0:T(8,128)(2,1)S(1)} custom-call(bf16[2,128,256]{2,1,0:T(8,128)(2,1)S(1)} %get-tuple-element.10.att, bf16[2,512,448]{2,1,0:T(8,128)(2,1)S(1)} %get-tuple-element.11.wp), custom_call_target="tpu_custom_call" | custom-call | tf_op jit(solution)/shard_map/project/pallas_call | solution.py:395
  83.2 0.2 multiply_reduce_fusion
  83.4 0.1 copy.26
  83.4 0.1 eq.42
  83.5 0.1 fusion.3
  83.6 0.2 select_reduce_fusion.1
  83.8 0.1 reduce_sum.39
  83.9 0.1 copy.28
  84.0 0.1 convert_reduce_fusion
  84.1 0.0 copy-done.10
  84.1 0.3 convolution_convert_fusion
  84.4 1.0 reshape.38.outg
  85.4 88.8 %experts.1 = bf16[16,2,7168]{2,1,0:T(2,128)(2,1)} custom-call(bf16[16,2,7168]{2,1,0:T(2,128)(2,1)} %reshape.38.outg, bf16[7168,128]{1,0:T(8,128)(2,1)} %bitcast.13, bf16[7168,128]{1,0:T(8,128)(2,1)} %bitcast.15, bf16[128,7168]{1,0:T(8,128)(2,1)} %bitcast.17, bf16[7168,128]{1,0:T(8,128)(2,1)} %copy-done.3, bf16[7168,128]{1,0:T(8,128)(2,1)} %copy-done.4, ...), custom_call_target="tpu_custom_call" | custom-call | tf_op jit(solution)/shard_map/experts/pallas_call | solution.py:540
  174.3 1.2 reshape.39
  175.4 0.0 copy-done.12
  175.5 0.1 select_reduce_fusion
  175.5 0.9 fusion
  (18 shorter events, 0.1 us)
Async XLA Ops:
  2.8 1.5 copy-start
  4.3 1.5 copy-start.1
  5.8 1.5 copy-start.2
  7.3 0.9 copy-start.6
  8.2 0.9 copy-start.7
  9.1 0.9 copy-start.8
  10.0 73.1 %copy-start.9 = (bf16[8,7168]{1,0:T(8,128)(2,1)S(1)}, bf16[8,7168]{1,0:T(8,128)(2,1)}, u32[]{:S(2)}) copy-start(bf16[8,7168]{1,0:T(8,128)(2,1)} %param.19) | copy-start | bytes 344068
  34.4 1.3 copy-start.3
  35.7 1.2 copy-start.4
  36.9 1.3 copy-start.5
  38.1 45.2 %copy-start.11 = (s32[8,2]{0,1:T(2,128)S(1)}, s32[8,2]{0,1:T(2,128)}, u32[]{:S(2)}) copy-start(s32[8,2]{0,1:T(2,128)} %param.21) | copy-start | bytes 196
  38.1 45.9 %copy-start.10 = (f32[7168]{0:T(1024)S(1)}, f32[7168]{0:T(1024)}, u32[]{:S(2)}) copy-start(f32[7168]{0:T(1024)} %param.20) | copy-start | bytes 86020
  85.4 90.0 %copy-start.12 = (f32[8,2]{0,1:T(2,128)S(1)}, f32[8,2]{0,1:T(2,128)}, u32[]{:S(2)}) copy-start(f32[8,2]{0,1:T(2,128)} %param.22) | copy-start | bytes 196

commit v2 on v1

--- a/solution.py
+++ b/solution.py
@@ -39,9 +39,9 @@
 
 
 def attention(
-    q, k, v, g, cw, wo, eg, eu, ed,
-    att, wpair, sg, su, sd,
-    kb, vb, qb, gb, hk, hv, cb, tb, ss, rs,
+    q, k, v, g, cw, wo,
+    att, wpair,
+    kb, vb, qb, gb, gs, hk, hv, cb, tb, ss, rs, ls,
 ):
     z, core, e = place()
     other = 1 - core
@@ -82,6 +82,13 @@
         for cp in halo:
             cp.start()
 
+    rows = pl.ds(pl.multiple_of(core * 448, 64), 448)
+    own = [
+        pltpu.make_async_copy(k.at[:, pl.ds(off, 256)], kb.at[2, core], ls.at[0]),
+        pltpu.make_async_copy(v.at[:, pl.ds(off, 256)], vb.at[2, core], ls.at[1]),
+        pltpu.make_async_copy(q.at[:, pl.ds(off, 256)], qb.at[core], ls.at[2]),
+        pltpu.make_async_copy(wo, wpair.at[rows], ls.at[3]),
+    ]
     swap = [
         rcopy(k.at[:, pl.ds(off_other, 256)], kb.at[2, core], ss.at[0], rs.at[0], sib),
         rcopy(v.at[:, pl.ds(off_other, 256)], vb.at[2, core], ss.at[1], rs.at[1], sib),
@@ -92,21 +99,17 @@
         cp.start()
     for cp in near:
         cp.start()
+    for cp in own:
+        cp.start()
     share = [
-        rcopy(wo, wpair.at[core], ss.at[4], rs.at[4], sib),
-        rcopy(eg, sg, ss.at[5], rs.at[5], sib),
-        rcopy(eu, su, ss.at[6], rs.at[6], sib),
-        rcopy(ed, sd, ss.at[7], rs.at[7], sib),
+        rcopy(wo, wpair.at[rows], ss.at[4], rs.at[4], sib),
     ]
     for cp in share:
         cp.start()
 
-    kb[2, core] = k[:, pl.ds(off, 256)]
-    vb[2, core] = v[:, pl.ds(off, 256)]
-    qb[core] = q[:, pl.ds(off, 256)]
     gb[core] = g[...]
-    wpair[core] = wo[...]
-
+    for cp in own:
+        cp.wait()
     for cp in swap:
         cp.wait_recv()
     halo[0].wait_recv()
@@ -157,7 +160,11 @@
     block_end = lax.broadcasted_iota(jnp.int32, (1, 128), 1) * 16 + 31
     key_pos = (z - 2) * 256 + lax.broadcasted_iota(jnp.int32, (1, 768), 1)
     lane = lax.broadcasted_iota(jnp.int32, (1, 128), 1)
-    gates = gb[...].reshape(256, 128)
+    gs[...] = jnp.zeros_like(gs)
+    for n in range(2):
+        gs[n, 0:4] = gb[n, 0]
+        gs[n, 4:8] = gb[n, 1]
+    gates = jnp.concatenate([gs[0].T, gs[1].T], 0)
     gates = 1.0 / (1.0 + jnp.exp(-gates))
     for h in range(2):
         hs = h * 128
@@ -193,24 +200,22 @@
         cp.wait()
 
 
-def run_attention(q, k, v, g, cw, wo, eg, eu, ed):
+def run_attention(q, k, v, g, cw, wo):
     vm = pl.BlockSpec(memory_space=pltpu.VMEM)
-    hbm = pl.BlockSpec(memory_space=pl.ANY)
+    hbm = pl.BlockSpec(memory_space=pltpu.HBM)
     return pl.pallas_call(
         attention,
         out_shape=(
             jax.ShapeDtypeStruct((2, 128, 256), BF),
-            jax.ShapeDtypeStruct((2, 512, 448), BF),
-            jax.ShapeDtypeStruct(eg.shape, BF),
-            jax.ShapeDtypeStruct(eu.shape, BF),
-            jax.ShapeDtypeStruct(ed.shape, BF),
+            jax.ShapeDtypeStruct((896, 512), BF),
         ),
-        in_specs=[vm] * 6 + [hbm] * 3,
-        out_specs=(vm, vm, hbm, hbm, hbm),
+        in_specs=[hbm] * 3 + [vm] * 2 + [hbm],
+        out_specs=(vm, vm),
         scratch_shapes=[
             pltpu.VMEM((3, 2, 128, 256), BF),
             pltpu.VMEM((3, 2, 128, 256), BF),
             pltpu.VMEM((2, 128, 256), BF),
+            pltpu.VMEM((2, 2, 4, 128), F32),
             pltpu.VMEM((2, 128, 128), F32),
             pltpu.VMEM((16, 256), BF),
             pltpu.VMEM((16, 256), BF),
@@ -218,12 +223,13 @@
             pltpu.VMEM((2, 128, 256), BF),
             pltpu.SemaphoreType.DMA((29,)),
             pltpu.SemaphoreType.DMA((29,)),
+            pltpu.SemaphoreType.DMA((4,)),
         ],
         compiler_params=pltpu.CompilerParams(
-            collective_id=1, has_side_effects=True, vmem_limit_bytes=32 << 20
+            collective_id=1, has_side_effects=True, vmem_limit_bytes=67043328
         ),
         name="attention",
-    )(q, k, v, g, cw, wo, eg, eu, ed)
+    )(q, k, v, g, cw, wo)
 
 
 def z_ring(buf, z, core, e, ss, rs):
@@ -265,34 +271,97 @@
                     sent.append(cp)
 
 
-def project(
-    att, wp,
-    hid,
-    xb, pb, a1, a2, a3, sb, c1, c2, c3, rb, ss, rs, s1, r1, s2, r2, s3, r3,
+DA = 4096
+DB = 7168 - DA
+NEAR = ((0, 1, 7, 2), (6, 3, 5, 4))
+
+
+def three(x):
+    a = x.astype(BF)
+    r = x - a.astype(F32)
+    b = r.astype(BF)
+    return jnp.concatenate([a, b, (r - b.astype(F32)).astype(BF)], 0)
+
+
+def turned(x):
+    if x.shape[0] < 128:
+        x = jnp.concatenate([x, jnp.zeros((128 - x.shape[0], 128), F32)], 0)
+    return x.T
+
+
+def one(cond):
+    return jnp.where(cond, 1.0, 0.0)
+
+
+def tail(
+    att, wp, res, gain, ids, gts, eg, eu, ed,
+    out,
+    sc, inf, hs, hid,
+    xb, pb, a1, a2, a3, sb, c1, c2, c3, rb, ss, rs, s1, r1, s2, r2, s3, r3, si, ri,
+    gw, dw, sw, rw, ls,
+    oa, aa, xa, ya, rv, mx, fs, ro, ra, tk, tr, sB, aB, yB, rB, zs, zr,
+    sa, qa, sg, qg, st, qt, sx, qx, sy, qy, sv, qv, sh, qh, sz, qz,
 ):
     z, core, e = place()
     ex, ey = lax.div(e, 4), lax.rem(e, 4)
     c = 2 * z + core
+    sib = (2 * z + 1 - core, e)
     ring = [
         (ex, lambda t: (c, 4 * lax.rem(t, 4) + ey)),
         (ey, lambda t: (c, 4 * ex + lax.rem(t, 4))),
     ]
     zp = [(2 * lax.rem(z + j, 8) + core, e) for j in range(1, 8)]
-    greet([dev(p + j) for p, dev in ring for j in (1, 3)] + zp)
+    plane = [(c, lax.rem(e + j, 16)) for j in range(1, 16)]
+    greet(plane + zp + [sib])
 
     xb[z] = att[...]
     copy, chunks = z_ring(xb, z, core, e, ss, rs)
     sent = []
     gather_start(copy, chunks, sent)
 
+    share = []
+    for n, src in enumerate((eg, eu)):
+        share.append(rcopy(src, gw.at[:, pl.ds(256 * n + 128, 128)], sw.at[n], rw.at[n], sib))
+    share.append(rcopy(ed, dw.at[pl.ds(128, 128), :], sw.at[2], rw.at[2], sib))
+    load = [
+        pltpu.make_async_copy(eg, gw.at[:, pl.ds(0, 128)], ls.at[0]),
+        pltpu.make_async_copy(eu, gw.at[:, pl.ds(256, 128)], ls.at[1]),
+        pltpu.make_async_copy(ed, dw.at[pl.ds(0, 128), :], ls.at[2]),
+    ]
+    for cp in share + load:
+        cp.start()
+
+    sc[...] = jnp.zeros_like(sc)
+    sc[0:2, 0:8] = ids[...].astype(F32)
+    sc[2:4, 0:8] = gts[...]
+    cols = sc[...].T
+    id0, id1, g0, g1 = (cols[0:8, n : n + 1] for n in range(4))
+    lane = lax.broadcasted_iota(jnp.int32, (8, 128), 1)
+    lanef = lane.astype(F32)
+    named = one(lanef == id0) + one(lanef == id1)
+    before, rows = jnp.zeros((1, 128), F32), []
+    for t in range(8):
+        rows.append(before)
+        before = before + named[t : t + 1]
+    count = jnp.concatenate(rows, 0)
+
+    def target(i):
+        return 2.0 * i + jnp.sum(jnp.where(lanef == i, count, 0.0), axis=1, keepdims=True)
+
+    t0, t1 = target(id0), target(id1)
+    inf[0] = jnp.where(
+        lane == 0, t0, jnp.where(lane == 1, t1, jnp.where(lane == 2, g0, jnp.where(lane == 3, g1, 0.0)))
+    )
+    told = [rcopy(inf.at[0], inf.at[8 - j], si.at[j], ri.at[j], zp[j - 1]) for j in range(1, 8)]
+    for cp in told:
+        cp.start()
+
     def partial(block, r):
         x0, x1 = xb[block, 0], xb[block, 1]
-        parts = [
-            jnp.dot(x0, wp[n, :256], preferred_element_type=F32)
-            + jnp.dot(x1, wp[n, 256:], preferred_element_type=F32)
-            for n in range(2)
-        ]
-        pb[r] = jnp.concatenate(parts, 1).reshape(4, 4, 8, 896).astype(BF)
+        dims = (((1,), (1,)), ((), ()))
+        y = lax.dot_general(x0, wp[:, :256], dims, preferred_element_type=F32)
+        y = y + lax.dot_general(x1, wp[:, 256:], dims, preferred_element_type=F32)
+        pb[r] = y.reshape(4, 4, 8, 896).astype(BF)
 
     partial(z, 0)
     for step in range(4):
@@ -371,7 +440,7 @@
         thin[half][0]()
     for r in thin:
         r[1]()
-    out = []
+    moved = []
     for half in range(2):
         lo, hi = thin[half][2]()
         rb[4 * half : 4 * half + 2] = lo.astype(BF)
@@ -380,24 +449,242 @@
             if j:
                 cp = rcopy(rb.at[j], hid.at[z], s3.at[j], r3.at[j], zp[j - 1])
                 cp.start()
-                out.append(cp)
+                moved.append(cp)
     hid[z] = rb[0]
-    for cp in out:
+
+    for cp in told:
+        cp.wait_recv()
+    mine0 = (lanef == t0) | (lanef == t1)
+    spread_a = turned(one(mine0))[:32, :16].astype(BF)
+    weigh_a = three((jnp.where(lanef == t0, g0, 0.0) + jnp.where(lanef == t1, g1, 0.0))[:, :32])
+    slot = lax.broadcasted_iota(jnp.int32, (32, 128), 1)
+    token = lax.broadcasted_iota(jnp.int32, (32, 128), 0)
+    slotf = (2 * lax.div(slot, 8) + lax.rem(slot, 2)).astype(F32)
+    same = lax.rem(lax.div(slot, 2), 4) == lax.div(token, 8)
+    spread_b, weigh_b = [], []
+    for g in range(2):
+        t = jnp.concatenate([inf[r] for r in NEAR[g]], 0)
+        hit0, hit1 = same & (slotf == t[:, 0:1]), same & (slotf == t[:, 1:2])
+        spread_b.append(turned(one(hit0 | hit1))[:, :32].astype(BF))
+        weigh_b.append(three(jnp.where(hit0, t[:, 2:3], 0.0) + jnp.where(hit1, t[:, 3:4], 0.0)))
+    pr = lax.broadcasted_iota(jnp.int32, (128, 128), 0)
+    pc = lax.broadcasted_iota(jnp.int32, (128, 128), 1)
+
+    def plane_place(n):
+        return lax.rem(lax.div(n, 2), 16) * 8 + lax.div(n, 32) * 2 + lax.rem(n, 2)
+
+    order = one(pc == plane_place(pr)).astype(BF)
+    unorder = one(pr == plane_place(pc)).astype(BF)
+
+    for cp in moved:
+        cp.wait_recv()
+    for n in range(8):
+        lo, hi = 896 * n, 896 * n + 896
+        hs[:, lo:hi] = res[:, lo:hi].astype(F32) + hid[n].astype(F32)
+    h = hs[...]
+    normed = h * lax.rsqrt(jnp.mean(h * h, axis=1, keepdims=True) + EPS) * gain[...]
+
+    tk[...] = normed[:, DA:].astype(BF)
+    tr[0] = tk[...]
+    spoke = []
+    for j in (1, 7, 2, 6, 3, 5, 4):
+        cp = rcopy(tk, tr.at[8 - j], st.at[j], qt.at[8 - j], zp[j - 1])
+        cp.start()
+        spoke.append(cp)
+
+    padded = jnp.concatenate([normed[:, :DA], jnp.zeros((8, DA), F32)], 0).astype(BF)
+    fs[...] = jnp.dot(spread_a, padded, preferred_element_type=F32)
+    for i in range(16):
+        oa[i] = fs[2 * i : 2 * i + 2, :].astype(BF)
+    go = []
+    for j in range(1, 16):
+        cp = rcopy(oa.at[lax.rem(e + j, 16)], aa.at[e], sa.at[j], qa.at[j], plane[j - 1])
+        cp.start()
+        go.append(cp)
+    aa[e] = oa[e]
+
+    def heard(r):
+        rcopy(tk, tr.at[r], st.at[0], qt.at[r], sib).wait_recv()
+
+    def scatter(g):
+        for r in NEAR[g]:
+            if r:
+                heard(r)
+        x = jnp.concatenate([tr[r].astype(F32) for r in NEAR[g]], 0).astype(BF)
+        y = jnp.dot(spread_b[g], x, preferred_element_type=F32)
+        sB[g] = y.reshape(16, 8, DB).astype(BF)
+        for j in range(1, 16):
+            cp = rcopy(
+                sB.at[g, lax.rem(e + j, 16)], aB.at[g, e], sg.at[g, j], qg.at[g, j], plane[j - 1]
+            )
+            cp.start()
+            go.append(cp)
+        aB[g, e] = sB[g, e]
+
+    scatter(0)
+    for cp in go[:15]:
+        cp.wait_recv()
+    for i in range(16):
+        fs[2 * i : 2 * i + 2, :] = aa[i].astype(F32)
+    xa[z, 0] = fs[0:16].astype(BF)
+    xa[z, 1] = fs[16:32].astype(BF)
+    copy2, chunks2 = z_ring(xa, z, core, e, sx, qx)
+    sent2 = []
+    gather_start(copy2, chunks2, sent2)
+    scatter(1)
+    for cp in load:
         cp.wait()
-    for cp in sent:
-        cp.wait_send()
+    for cp in share:
+        cp.wait_recv()
+
+    home = []
+
+    def work(g):
+        blocks = [lax.rem(z + r, 8) for r in NEAR[g]]
+        x = jnp.concatenate([xa[b, n] for b in blocks for n in range(2)], 0)
+        y = jnp.dot(x, gw[0:DA, :], preferred_element_type=F32)
+        for j in range(1, 16):
+            rcopy(sB.at[g, 0], aB.at[g, 0], sg.at[g, j], qg.at[g, j], sib).wait_recv()
+        x = aB[g].astype(F32).reshape(128, DB).astype(BF)
+        x = jnp.dot(order, x, preferred_element_type=F32).astype(BF)
+        y = y + jnp.dot(x, gw[DA:, :], preferred_element_type=F32)
+        gate, lift = y[:, :256], y[:, 256:]
+        act = (gate / (1.0 + jnp.exp(-gate)) * lift).astype(BF)
+        actp = jnp.dot(unorder, act, preferred_element_type=F32).astype(BF)
+
+        @pl.loop(0, DB // 512)
+        def _(n):
+            cols = pl.ds(pl.multiple_of(n * 512, 512), 512)
+            dcols = pl.ds(pl.multiple_of(DA + n * 512, 512), 512)
+            y = jnp.dot(actp, dw[:, dcols], preferred_element_type=F32)
+            yB[g, :, :, cols] = y.reshape(16, 8, 512).astype(BF)
+
+        for j in range(1, 16):
+            cp = rcopy(
+                yB.at[g, lax.rem(e + j, 16)], rB.at[g, e], sy.at[g, j], qy.at[g, j], plane[j - 1]
+            )
+            cp.start()
+            home.append(cp)
+        rB[g, e] = yB[g, e]
+
+        @pl.loop(0, DA // 512)
+        def _(n):
+            cols = pl.ds(pl.multiple_of(n * 512, 512), 512)
+            y = jnp.dot(act, dw[:, cols], preferred_element_type=F32).astype(BF)
+            for i, b in enumerate(blocks):
+                ya[b, 0, :, cols] = y[32 * i : 32 * i + 16]
+                ya[b, 1, :, cols] = y[32 * i + 16 : 32 * i + 32]
+
+    gather_step(copy2, chunks2, 0, sent2)
+    gather_step(copy2, chunks2, 1, sent2)
+    work(0)
+    gather_step(copy2, chunks2, 2, sent2)
+    gather_step(copy2, chunks2, 3, sent2)
+    work(1)
+
+    up, down = zp[0], zp[6]
+
+    def leg(way, n, src):
+        return rcopy(
+            src, rv.at[way, n], sv.at[way * 7 + n], qv.at[way * 7 + n], up if way == 0 else down
+        )
+
+    def mine(way, dist, first):
+        block = lax.rem(z + dist, 8) if way == 0 else lax.rem(z + 8 - dist, 8)
+        return ya.at[block, first if way == 0 else 1 - first]
+
+    back = []
+
+    def send(way, n, src):
+        cp = leg(way, n, src)
+        cp.start()
+        back.append(cp)
+
+    for way in (0, 1):
+        send(way, 0, mine(way, 4, 0))
+    for way in (0, 1):
+        send(way, 2, mine(way, 3, 1))
+
+    def along(n, dist, first, source):
+        for way in (0, 1):
+            leg(way, source, rv.at[way, source]).wait_recv()
+            mx[way, n] = (
+                rv[way, source].astype(F32) + mine(way, dist, first)[...].astype(F32)
+            ).astype(BF)
+            send(way, n, mx.at[way, n])
+
+    part = []
+
+    def gather_home(g):
+        for j in range(1, 16):
+            rcopy(yB.at[g, 0], rB.at[g, 0], sy.at[g, j], qy.at[g, j], sib).wait_recv()
+        x = rB[g].astype(F32).reshape(128, DB).astype(BF)
+        y = jnp.dot(weigh_b[g], x, preferred_element_type=F32)
+        y = y[0:32] + y[32:64] + y[64:96]
+        for i, r in enumerate(NEAR[g]):
+            zs[r] = y[8 * i : 8 * i + 8].astype(BF)
+            if r:
+                cp = rcopy(zs.at[r], zr.at[8 - r], sz.at[r], qz.at[8 - r], zp[r - 1])
+                cp.start()
+                part.append(cp)
+
+    along(1, 3, 0, 0)
+    along(3, 2, 0, 1)
+    along(4, 2, 1, 2)
+    gather_home(0)
+    along(5, 1, 0, 3)
+    along(6, 1, 1, 4)
+    for chunk in range(2):
+        total = ya[z, chunk].astype(F32)
+        for way in (0, 1):
+            n = 5 + (chunk if way == 0 else 1 - chunk)
+            leg(way, n, rv.at[way, n]).wait_recv()
+            total = total + rv[way, n].astype(F32)
+        fs[16 * chunk : 16 * chunk + 16] = total
+    for i in range(16):
+        ro[i] = fs[2 * i : 2 * i + 2, :].astype(BF)
+    last = []
+    for j in range(1, 16):
+        cp = rcopy(ro.at[lax.rem(e + j, 16)], ra.at[e], sh.at[j], qh.at[j], plane[j - 1])
+        cp.start()
+        last.append(cp)
+    ra[e] = ro[e]
+    gather_home(1)
+    for cp in last:
+        cp.wait_recv()
+    for i in range(16):
+        fs[2 * i : 2 * i + 2, :] = ra[i].astype(F32)
+    y = jnp.dot(weigh_a, fs[...].astype(BF), preferred_element_type=F32)
+    out[:, :DA] = (hs[:, :DA] + (y[0:8] + y[8:16] + y[16:24])).astype(BF)
+    total = hs[:, DA:] + zs[0].astype(F32)
+    for r in range(1, 8):
+        rcopy(zs.at[0], zr.at[r], sz.at[0], qz.at[r], sib).wait_recv()
+        total = total + zr[r].astype(F32)
+    out[:, DA:] = total.astype(BF)
+
     for r in wide + thin:
         r[3]()
-
-
-def run_project(att, wp):
+    for cp in sent + share + told + moved + spoke + go + sent2 + home + back + part + last:
+        cp.wait_send()
+
+
+def run_tail(att, wp, res, gain, ids, gts, eg, eu, ed):
     vm = pl.BlockSpec(memory_space=pltpu.VMEM)
+    hbm = pl.BlockSpec(memory_space=pltpu.HBM)
+
+    def dma(*shape):
+        return pltpu.SemaphoreType.DMA(shape)
+
     return pl.pallas_call(
-        project,
-        out_shape=jax.ShapeDtypeStruct((8, 8, 896), BF),
-        in_specs=[vm] * 2,
+        tail,
+        out_shape=jax.ShapeDtypeStruct((8, 7168), BF),
+        in_specs=[vm] * 6 + [hbm] * 3,
         out_specs=vm,
         scratch_shapes=[
+            pltpu.VMEM((128, 128), F32),
+            pltpu.VMEM((8, 8, 128), F32),
+            pltpu.VMEM((8, 7168), F32),
+            pltpu.VMEM((8, 8, 896), BF),
             pltpu.VMEM((8, 2, 128, 256), BF),
             pltpu.VMEM((8, 4, 4, 8, 896), BF),
             pltpu.VMEM((2, 2, 2, 4, 8, 896), BF),
@@ -408,165 +695,35 @@
             pltpu.VMEM((2, 2, 4, 8, 896), BF),
             pltpu.VMEM((2, 2, 2, 8, 896), BF),
             pltpu.VMEM((8, 8, 896), BF),
-            pltpu.SemaphoreType.DMA((14,)),
-            pltpu.SemaphoreType.DMA((14,)),
-            pltpu.SemaphoreType.DMA((12,)),
-            pltpu.SemaphoreType.DMA((12,)),
-            pltpu.SemaphoreType.DMA((12,)),
-            pltpu.SemaphoreType.DMA((12,)),
-            pltpu.SemaphoreType.DMA((8,)),
-            pltpu.SemaphoreType.DMA((8,)),
+            dma(14), dma(14), dma(12), dma(12), dma(12), dma(12), dma(8), dma(8), dma(8), dma(8),
+            pltpu.VMEM((7168, 512), BF),
+            pltpu.VMEM((256, 7168), BF),
+            dma(3), dma(3), dma(3),
+            pltpu.VMEM((16, 2, DA), BF),
+            pltpu.VMEM((16, 2, DA), BF),
+            pltpu.VMEM((8, 2, 16, DA), BF),
+            pltpu.VMEM((8, 2, 16, DA), BF),
+            pltpu.VMEM((2, 7, 16, DA), BF),
+            pltpu.VMEM((2, 7, 16, DA), BF),
+            pltpu.VMEM((32, DA), F32),
+            pltpu.VMEM((16, 2, DA), BF),
+            pltpu.VMEM((16, 2, DA), BF),
+            pltpu.VMEM((8, DB), BF),
+            pltpu.VMEM((8, 8, DB), BF),
+            pltpu.VMEM((2, 16, 8, DB), BF),
+            pltpu.VMEM((2, 16, 8, DB), BF),
+            pltpu.VMEM((2, 16, 8, DB), BF),
+            pltpu.VMEM((2, 16, 8, DB), BF),
+            pltpu.VMEM((8, 8, DB), BF),
+            pltpu.VMEM((8, 8, DB), BF),
+            dma(16), dma(16), dma(2, 16), dma(2, 16), dma(8), dma(8), dma(14), dma(14),
+            dma(2, 16), dma(2, 16), dma(14), dma(14), dma(16), dma(16), dma(8), dma(8),
         ],
         compiler_params=pltpu.CompilerParams(
-            collective_id=2, has_side_effects=True, vmem_limit_bytes=40 << 20
+            collective_id=2, has_side_effects=True, vmem_limit_bytes=67043328
         ),
-        name="project",
-    )(att, wp)
-
-
-def experts(
-    outg, eg, eu, ed, sg, su, sd,
-    ret,
-    gw, dw, arr, xb, ob, rv, mx, fs, ro, ls, s0, r0, ss, rs, s1, r1, s2, r2,
-):
-    z, core, e = place()
-    c = 2 * z + core
-    up, down = (2 * lax.rem(z + 1, 8) + core, e), (2 * lax.rem(z + 7, 8) + core, e)
-    plane = [(c, lax.rem(e + j, 16)) for j in range(1, 16)]
-    greet(plane + [up, down])
-
-    go = []
-    for j in range(1, 16):
-        cp = rcopy(outg.at[lax.rem(e + j, 16)], arr.at[e], s0.at[j], r0.at[j], plane[j - 1])
-        cp.start()
-        go.append(cp)
-    load = [
-        pltpu.make_async_copy(src, gw.at[:, pl.ds(128 * n, 128)], ls.at[n])
-        for n, src in enumerate((eg, sg, eu, su))
-    ] + [
-        pltpu.make_async_copy(src, dw.at[pl.ds(128 * n, 128), :], ls.at[4 + n])
-        for n, src in enumerate((ed, sd))
-    ]
-    for cp in load:
-        cp.start()
-    arr[e] = outg[e]
-    for cp in go:
-        cp.wait_recv()
-    for i in range(16):
-        fs[2 * i : 2 * i + 2, :] = arr[i].astype(F32)
-    xb[z, 0] = fs[0:16].astype(BF)
-    xb[z, 1] = fs[16:32].astype(BF)
-
-    copy, chunks = z_ring(xb, z, core, e, ss, rs)
-    sent = []
-    gather_start(copy, chunks, sent)
-    for cp in load:
-        cp.wait()
-
-    def work(a, b):
-        x = jnp.concatenate([xb[a, 0], xb[a, 1], xb[b, 0], xb[b, 1]], 0)
-        y = jnp.dot(x, gw[...], preferred_element_type=F32)
-        gate, lift = y[:, :256], y[:, 256:]
-        act = (gate / (1.0 + jnp.exp(-gate)) * lift).astype(BF)
-
-        @pl.loop(0, 7)
-        def _(n):
-            cols = pl.ds(pl.multiple_of(n * 1024, 1024), 1024)
-            out = jnp.dot(act, dw[:, cols], preferred_element_type=F32).astype(BF)
-            ob[a, 0, :, cols] = out[0:16]
-            ob[a, 1, :, cols] = out[16:32]
-            ob[b, 0, :, cols] = out[32:48]
-            ob[b, 1, :, cols] = out[48:64]
-
-    for step in range(4):
-        gather_step(copy, chunks, step, sent)
-        if step < 3:
-            work(lax.rem(z + step + 1, 8), lax.rem(z + 7 - step, 8))
-        else:
-            work(lax.rem(z + 4, 8), z)
-
-    def leg(way, slot, src):
-        return rcopy(
-            src, rv.at[way, slot], s1.at[way * 7 + slot], r1.at[way * 7 + slot], up if way == 0 else down
-        )
-
-    def mine(way, dist, first):
-        block = lax.rem(z + dist, 8) if way == 0 else lax.rem(z + 8 - dist, 8)
-        chunk = first if way == 0 else 1 - first
-        return ob.at[block, chunk]
-
-    back = []
-
-    def send(way, slot, src):
-        cp = leg(way, slot, src)
-        cp.start()
-        back.append(cp)
-
-    for way in (0, 1):
-        send(way, 0, mine(way, 4, 0))
-    for way in (0, 1):
-        send(way, 2, mine(way, 3, 1))
-    for slot, dist, first, source in ((1, 3, 0, 0), (3, 2, 0, 1), (4, 2, 1, 2), (5, 1, 0, 3), (6, 1, 1, 4)):
-        for way in (0, 1):
-            leg(way, source, rv.at[way, source]).wait_recv()
-            mx[way, slot] = (
-                rv[way, source].astype(F32) + mine(way, dist, first)[...].astype(F32)
-            ).astype(BF)
-            send(way, slot, mx.at[way, slot])
-    for chunk in range(2):
-        total = ob[z, chunk].astype(F32)
-        for way in (0, 1):
-            slot = 5 + (chunk if way == 0 else 1 - chunk)
-            leg(way, slot, rv.at[way, slot]).wait_recv()
-            total = total + rv[way, slot].astype(F32)
-        fs[16 * chunk : 16 * chunk + 16] = total
-    for i in range(16):
-        ro[i] = fs[2 * i : 2 * i + 2, :].astype(BF)
-    home = []
-    for j in range(1, 16):
-        cp = rcopy(ro.at[lax.rem(e + j, 16)], ret.at[e], s2.at[j], r2.at[j], plane[j - 1])
-        cp.start()
-        home.append(cp)
-    ret[e] = ro[e]
-    for cp in home:
-        cp.wait()
-    for cp in go + sent + back:
-        cp.wait_send()
-
-
-def run_experts(outg, eg, eu, ed, sg, su, sd):
-    vm = pl.BlockSpec(memory_space=pltpu.VMEM)
-    hbm = pl.BlockSpec(memory_space=pl.ANY)
-    return pl.pallas_call(
-        experts,
-        out_shape=jax.ShapeDtypeStruct((16, 2, 7168), BF),
-        in_specs=[vm] + [hbm] * 6,
-        out_specs=vm,
-        scratch_shapes=[
-            pltpu.VMEM((7168, 512), BF),
-            pltpu.VMEM((256, 7168), BF),
-            pltpu.VMEM((16, 2, 7168), BF),
-            pltpu.VMEM((8, 2, 16, 7168), BF),
-            pltpu.VMEM((8, 2, 16, 7168), BF),
-            pltpu.VMEM((2, 7, 16, 7168), BF),
-            pltpu.VMEM((2, 7, 16, 7168), BF),
-            pltpu.VMEM((32, 7168), F32),
-            pltpu.VMEM((16, 2, 7168), BF),
-            pltpu.SemaphoreType.DMA((6,)),
-            pltpu.SemaphoreType.DMA((16,)),
-            pltpu.SemaphoreType.DMA((16,)),
-            pltpu.SemaphoreType.DMA((14,)),
-            pltpu.SemaphoreType.DMA((14,)),
-            pltpu.SemaphoreType.DMA((14,)),
-            pltpu.SemaphoreType.DMA((14,)),
-            pltpu.SemaphoreType.DMA((16,)),
-            pltpu.SemaphoreType.DMA((16,)),
-        ],
-        compiler_params=pltpu.CompilerParams(
-            collective_id=3, has_side_effects=True, vmem_limit_bytes=58 << 20
-        ),
-        name="experts",
-    )(outg, eg, eu, ed, sg, su, sd)
+        name="tail",
+    )(att, wp, res, gain, ids, gts, eg, eu, ed)
 
 
 def local(
@@ -584,38 +741,13 @@
     expert_up,
     expert_down,
 ):
-    gates = jnp.pad(gate_logits.transpose(1, 0, 2).reshape(128, 8), ((0, 0), (0, 120)))
+    gates = gate_logits.transpose(0, 2, 1)
     cw = jnp.broadcast_to(comp_weight.transpose(0, 2, 1)[..., None], (2, 4, 32, 128))
-    att, wpair, sg, su, sd = run_attention(
-        query_input, key_input, value_input, gates, cw, out_proj,
+    att, wpair = run_attention(query_input, key_input, value_input, gates, cw, out_proj.T)
+    return run_tail(
+        att, wpair, residual_in, ffn_gain.reshape(1, 7168), expert_ids.T, route_gates.T,
         expert_gate[0], expert_up[0], expert_down[0],
     )
-    projected = run_project(att, wpair)
-    projected = projected.transpose(1, 0, 2).reshape(8, 7168).astype(F32)
-    hidden_state = residual_in.astype(F32) + projected
-    mean_square = jnp.mean(hidden_state * hidden_state, axis=1, keepdims=True)
-    normed = (hidden_state * lax.rsqrt(mean_square + EPS) * ffn_gain).astype(BF)
-
-    flat_ids = expert_ids.reshape(-1)
-    chosen = (flat_ids[:, None] == jnp.arange(16, dtype=jnp.int32)[None, :]).astype(jnp.int32)
-    slots = jnp.sum((jnp.cumsum(chosen, axis=0) - chosen) * chosen, axis=1)
-    targets = (flat_ids * 2 + slots).reshape(8, 2)
-    slot_range = jnp.arange(32, dtype=jnp.int32)
-    dispatch_map = jnp.sum(
-        (slot_range[:, None, None] == targets[None, :, :]).astype(F32), axis=2
-    ).astype(BF)
-    outgoing = (
-        jnp.dot(dispatch_map, normed, preferred_element_type=F32).astype(BF).reshape(16, 2, 7168)
-    )
-    returned = run_experts(
-        outgoing, expert_gate[0], expert_up[0], expert_down[0], sg, su, sd
-    ).reshape(32, 7168)
-    combine_map = jnp.sum(
-        jnp.where(slot_range[None, None, :] == targets[:, :, None], route_gates[:, :, None], 0.0),
-        axis=1,
-    )
-    moe_out = jnp.dot(combine_map, returned.astype(F32), precision=lax.Precision.HIGHEST)
-    return (hidden_state + moe_out).astype(BF)
 
 
 def solution(mesh):

time: 178 us -> 151 us (0.85)
  local copies, waits for them, and re-layouts: 16.2 us -> 2.99 us
  Pallas kernels: 158 us -> 146 us
    pallas_call x2 -> x1, Pallas kernels: 134 us -> 119 us  [run_tail(): pl.pallas_call(tail, out_shape=jax.ShapeDtypeStruct((8, 7168), BF), in_sp...]
    unnamed x28 -> x1, local copies, waits for them, and re-layouts: 12.2 us -> 1.55 us
    reshape x3 -> x0, local copies, waits for them, and re-layouts: 2.97 us -> none  [the longest x1 1.19 us: local(): returned = run_experts(outgoing, expert_gate[0], expert_up[0], expert_dow...]
    pallas_call x1, Pallas kernels: 24.4 us -> 26.6 us  [run_attention(): pl.pallas_call(attention, out_shape=(jax.ShapeDtypeStruct((2, 128, 256),...]
where the time goes in v2:
time: 151 us; the launch traced here: 149 us
  Pallas kernels  146 us (97%)
  local copies, waits for them, and re-layouts  2.99 us (2%)
    pallas_call x1, Pallas kernels, run_tail(): pl.pallas_call(tail, out_shape=jax.ShapeDtypeStruct((8, 7168), BF), in_sp...  119 us
    pallas_call x1, Pallas kernels, run_attention(): pl.pallas_call(attention, out_shape=(jax.ShapeDtypeStruct((2, 128, 256),...  26.6 us

profile of v2, /device:TPU:32, one launch (start us, length us, event | category | flops | bytes accessed | tf_op | source)
XLA Modules:
  0.0 148.8 jit_solution(2897838232231922609)
XLA Ops:
  0.0 1.4 broadcast_in_dim.2.cw
  1.4 26.6 %attention.1 = (bf16[2,128,256]{2,1,0:T(8,128)(2,1)}, bf16[896,512]{1,0:T(8,128)(2,1)}) custom-call(bf16[128,512]{1,0:T(8,128)(2,1)} %q.1, bf16[128,512]{1,0:T(8,128)(2,1)} %k.1, bf16[128,512]{1,0:T(8,128)(2,1)} %v.1, f32[2,4,128]{2,1,0:T(4,128)} %bitcast.14, f32[2,4,32,128]{3,2,1,0:T(8,128)} %broadcast_in_dim.2.cw, bf16[448,512]{1,0:T(8,128)(2,1)} %bitcast.12), custom_call_target="tpu_custom_call" | custom-call | tf_op jit(solution)/shard_map/attention/pallas_call | solution.py:206
  28.0 119.2 %tail.1 = bf16[8,7168]{1,0:T(8,128)(2,1)} custom-call(bf16[2,128,256]{2,1,0:T(8,128)(2,1)} %get-tuple-element.7.att, bf16[896,512]{1,0:T(8,128)(2,1)} %get-tuple-element.8.wp, bf16[8,7168]{1,0:T(8,128)(2,1)} %res.1, f32[1,7168]{1,0:T(1,128)} %bitcast.13, s32[2,8]{1,0:T(2,128)} %bitcast.16, f32[2,8]{1,0:T(2,128)} %bitcast.17, bf16[7168,128]{1,0:T(8,128)(2,1)} %bitcast.9, ...), custom_call_target="tpu_custom_call" | custom-call | tf_op jit(solution)/shard_map/tail/pallas_call | solution.py:678
  147.2 1.6 %copy.15 = bf16[8,7168]{1,0:T(8,128)(2,1)} copy(bf16[8,7168]{1,0:T(8,128)(2,1)} %tail.1) | data formatting | bytes 229376

commit v3 on v2

--- a/solution.py
+++ b/solution.py
@@ -38,18 +38,11 @@
     return x * lax.rsqrt(jnp.mean(x * x, axis=1, keepdims=True) + EPS)
 
 
-def attention(
-    q, k, v, g, cw, wo,
-    att, wpair,
-    kb, vb, qb, gb, gs, hk, hv, cb, tb, ss, rs, ls,
-):
-    z, core, e = place()
+def attend(z, core, e, q, k, v, g, cw, wo, wpair, xb, kb, vb, qb, gb, gs, hk, hv, cb, tb, ss, rs, ls):
     other = 1 - core
     up, down = lax.rem(z + 1, 8), lax.rem(z + 7, 8)
     sib = (2 * z + other, e)
     peers = [(2 * lax.rem(z + j, 8) + core, e) for j in range(1, 8)]
-    greet([sib, (2 * up + other, e), (2 * down + other, e)] + peers)
-
     off_other = pl.multiple_of(other * 256, 256)
     off = pl.multiple_of(core * 256, 256)
     near = []
@@ -108,14 +101,29 @@
         cp.start()
 
     gb[core] = g[...]
-    for cp in own:
-        cp.wait()
-    for cp in swap:
-        cp.wait_recv()
-    halo[0].wait_recv()
-    halo[1].wait_recv()
-
-    for a, (blocks, tail) in enumerate(((kb, hk), (vb, hv))):
+
+    relay = []
+
+    def pass_on(n):
+        for a, buf in enumerate((kb, vb)):
+            rcopy(buf.at[1, n], buf.at[1, n], ss.at[8], rs.at[8 + 2 * n + a], sib).wait_recv()
+            cp = rcopy(
+                buf.at[1, n],
+                buf.at[0, n],
+                ss.at[12 + 2 * n + a],
+                rs.at[12 + 2 * n + a],
+                (2 * up + core, e),
+            )
+            cp.start()
+            relay.append(cp)
+
+    gs[...] = jnp.zeros_like(gs)
+    gs[0, 0:4, 0:32] = cw[0]
+    gs[0, 4:8, 0:32] = cw[1]
+    weights = gs[0].T[0:32]
+    lane = lax.broadcasted_iota(jnp.int32, (1, 128), 1)
+
+    def squeeze(a, blocks, tail):
         for h in range(2):
             hs = h * 128
             last = jnp.where(z == 7, 0.0, tail[:, hs : hs + 128].astype(F32))
@@ -127,30 +135,28 @@
                 ],
                 0,
             ).reshape(17, 16, 128)
-            w = cw[a, 2 * core + h]
+            w = jnp.sum(jnp.where(lane == 4 * a + 2 * core + h, weights, 0.0), axis=1, keepdims=True)
+            w = jnp.broadcast_to(w, (32, 128))
             y = jnp.sum(x[:16] * w[None, :16], axis=1) + jnp.sum(x[1:] * w[None, 16:], axis=1)
             if a == 0:
                 y = unit(y)
             cb[z, a, :, hs : hs + 128] = y.astype(BF)
+
+    for cp in own:
+        cp.wait()
+    pass_on(0)
+    for cp in swap:
+        cp.wait_recv()
+    for cp in halo[:2]:
+        cp.wait_recv()
+    squeeze(0, kb, hk)
+    pass_on(1)
+    squeeze(1, vb, hv)
     comps = [
         rcopy(cb.at[z], cb.at[z], ss.at[20 + j], rs.at[20 + j], peers[j - 1]) for j in range(1, 8)
     ]
     for cp in comps:
         cp.start()
-
-    relay = []
-    for s in range(2):
-        for a, buf in enumerate((kb, vb)):
-            rcopy(buf.at[1, s], buf.at[1, s], ss.at[8], rs.at[8 + 2 * s + a], sib).wait_recv()
-            cp = rcopy(
-                buf.at[1, s],
-                buf.at[0, s],
-                ss.at[12 + 2 * s + a],
-                rs.at[12 + 2 * s + a],
-                (2 * up + core, e),
-            )
-            cp.start()
-            relay.append(cp)
     for cp in comps:
         cp.wait_recv()
     for cp in relay:
@@ -159,8 +165,6 @@
     pos = z * 256 + lax.broadcasted_iota(jnp.int32, (256, 1), 0)
     block_end = lax.broadcasted_iota(jnp.int32, (1, 128), 1) * 16 + 31
     key_pos = (z - 2) * 256 + lax.broadcasted_iota(jnp.int32, (1, 768), 1)
-    lane = lax.broadcasted_iota(jnp.int32, (1, 128), 1)
-    gs[...] = jnp.zeros_like(gs)
     for n in range(2):
         gs[n, 0:4] = gb[n, 0]
         gs[n, 4:8] = gb[n, 1]
@@ -185,62 +189,31 @@
         g1 = jnp.sum(jnp.where(lane == 2 * core + h, gates, 0.0), axis=1, keepdims=True)
         g2 = jnp.sum(jnp.where(lane == 4 + 2 * core + h, gates, 0.0), axis=1, keepdims=True)
         tb[:, :, hs : hs + 128] = (g1 * o1 + g2 * o2).astype(BF).reshape(2, 128, 128)
-    back = rcopy(tb.at[other], att.at[core], ss.at[28], rs.at[28], sib)
+    back = rcopy(tb.at[other], xb.at[z, core], ss.at[28], rs.at[28], sib)
     back.start()
-    att[core] = tb[core]
-
-    @pl.when(core == 0)
-    def _():
-        for cp in halo:
+    xb[z, core] = tb[core]
+
+    def drain():
+        @pl.when(core == 0)
+        def _():
+            for cp in halo:
+                cp.wait_send()
+
+        for cp in swap + near + comps + relay + share + [back]:
             cp.wait_send()
 
-    for cp in swap + near + comps + relay:
-        cp.wait_send()
-    for cp in share + [back]:
-        cp.wait()
-
-
-def run_attention(q, k, v, g, cw, wo):
-    vm = pl.BlockSpec(memory_space=pltpu.VMEM)
-    hbm = pl.BlockSpec(memory_space=pltpu.HBM)
-    return pl.pallas_call(
-        attention,
-        out_shape=(
-            jax.ShapeDtypeStruct((2, 128, 256), BF),
-            jax.ShapeDtypeStruct((896, 512), BF),
-        ),
-        in_specs=[hbm] * 3 + [vm] * 2 + [hbm],
-        out_specs=(vm, vm),
-        scratch_shapes=[
-            pltpu.VMEM((3, 2, 128, 256), BF),
-            pltpu.VMEM((3, 2, 128, 256), BF),
-            pltpu.VMEM((2, 128, 256), BF),
-            pltpu.VMEM((2, 2, 4, 128), F32),
-            pltpu.VMEM((2, 128, 128), F32),
-            pltpu.VMEM((16, 256), BF),
-            pltpu.VMEM((16, 256), BF),
-            pltpu.VMEM((8, 2, 16, 256), BF),
-            pltpu.VMEM((2, 128, 256), BF),
-            pltpu.SemaphoreType.DMA((29,)),
-            pltpu.SemaphoreType.DMA((29,)),
-            pltpu.SemaphoreType.DMA((4,)),
-        ],
-        compiler_params=pltpu.CompilerParams(
-            collective_id=1, has_side_effects=True, vmem_limit_bytes=67043328
-        ),
-        name="attention",
-    )(q, k, v, g, cw, wo)
-
-
-def z_ring(buf, z, core, e, ss, rs):
+    return share[0], back, drain
+
+
+def z_ring(buf, z, core, e, ss, rs, turn):
     up, down = lax.rem(z + 1, 8), lax.rem(z + 7, 8)
 
     def copy(way, step, chunk):
         block = lax.rem(z + 8 - step, 8) if way == 0 else lax.rem(z + step, 8)
         slot = way * 7 + 2 * step + (chunk if step < 3 else 0)
         return rcopy(
-            buf.at[block, chunk],
-            buf.at[block, chunk],
+            buf.at[block, lax.rem(chunk + turn, 2)],
+            buf.at[block, lax.rem(chunk + turn, 2)],
             ss.at[slot],
             rs.at[slot],
             (2 * (up if way == 0 else down) + core, e),
@@ -252,12 +225,11 @@
     return copy, chunks
 
 
-def gather_start(copy, chunks, sent):
-    for chunk in (0, 1):
-        for way in (0, 1):
-            cp = copy(way, 0, chunk)
-            cp.start()
-            sent.append(cp)
+def gather_start(copy, chunk, sent):
+    for way in (0, 1):
+        cp = copy(way, 0, chunk)
+        cp.start()
+        sent.append(cp)
 
 
 def gather_step(copy, chunks, step, sent):
@@ -273,6 +245,8 @@
 
 DA = 4096
 DB = 7168 - DA
+HA = 3584
+HB = 7168 - HA
 NEAR = ((0, 1, 7, 2), (6, 3, 5, 4))
 
 
@@ -294,8 +268,9 @@
 
 
 def tail(
-    att, wp, res, gain, ids, gts, eg, eu, ed,
+    q, k, v, g, cw, wo, res, gain, ids, gts, eg, eu, ed,
     out,
+    wp, kb, vb, qb, gb, gs, hk, hv, cb, tb, s0, r0, l0,
     sc, inf, hs, hid,
     xb, pb, a1, a2, a3, sb, c1, c2, c3, rb, ss, rs, s1, r1, s2, r2, s3, r3, si, ri,
     gw, dw, sw, rw, ls,
@@ -312,12 +287,15 @@
     ]
     zp = [(2 * lax.rem(z + j, 8) + core, e) for j in range(1, 8)]
     plane = [(c, lax.rem(e + j, 16)) for j in range(1, 16)]
-    greet(plane + zp + [sib])
-
-    xb[z] = att[...]
-    copy, chunks = z_ring(xb, z, core, e, ss, rs)
+    cross = [(2 * lax.rem(z + j, 8) + 1 - core, e) for j in (1, 7)]
+    greet(plane + zp + [sib] + cross)
+    outw, swapped, drain = attend(
+        z, core, e, q, k, v, g, cw, wo, wp, xb, kb, vb, qb, gb, gs, hk, hv, cb, tb, s0, r0, l0
+    )
+
+    copy, chunks = z_ring(xb, z, core, e, ss, rs, core)
     sent = []
-    gather_start(copy, chunks, sent)
+    gather_start(copy, 0, sent)
 
     share = []
     for n, src in enumerate((eg, eu)):
@@ -363,6 +341,9 @@
         y = y + lax.dot_general(x1, wp[:, 256:], dims, preferred_element_type=F32)
         pb[r] = y.reshape(4, 4, 8, 896).astype(BF)
 
+    swapped.wait_recv()
+    gather_start(copy, 1, sent)
+    outw.wait_recv()
     partial(z, 0)
     for step in range(4):
         gather_step(copy, chunks, step, sent)
@@ -493,9 +474,9 @@
         spoke.append(cp)
 
     padded = jnp.concatenate([normed[:, :DA], jnp.zeros((8, DA), F32)], 0).astype(BF)
-    fs[...] = jnp.dot(spread_a, padded, preferred_element_type=F32)
+    fs[:, :DA] = jnp.dot(spread_a, padded, preferred_element_type=F32)
     for i in range(16):
-        oa[i] = fs[2 * i : 2 * i + 2, :].astype(BF)
+        oa[i] = fs[2 * i : 2 * i + 2, :DA].astype(BF)
     go = []
     for j in range(1, 16):
         cp = rcopy(oa.at[lax.rem(e + j, 16)], aa.at[e], sa.at[j], qa.at[j], plane[j - 1])
@@ -525,12 +506,13 @@
     for cp in go[:15]:
         cp.wait_recv()
     for i in range(16):
-        fs[2 * i : 2 * i + 2, :] = aa[i].astype(F32)
-    xa[z, 0] = fs[0:16].astype(BF)
-    xa[z, 1] = fs[16:32].astype(BF)
-    copy2, chunks2 = z_ring(xa, z, core, e, sx, qx)
+        fs[2 * i : 2 * i + 2, :DA] = aa[i].astype(F32)
+    xa[z, 0] = fs[0:16, :DA].astype(BF)
+    xa[z, 1] = fs[16:32, :DA].astype(BF)
+    copy2, chunks2 = z_ring(xa, z, core, e, sx, qx, 0)
     sent2 = []
-    gather_start(copy2, chunks2, sent2)
+    gather_start(copy2, 0, sent2)
+    gather_start(copy2, 1, sent2)
     scatter(1)
     for cp in load:
         cp.wait()
@@ -552,10 +534,10 @@
         act = (gate / (1.0 + jnp.exp(-gate)) * lift).astype(BF)
         actp = jnp.dot(unorder, act, preferred_element_type=F32).astype(BF)
 
-        @pl.loop(0, DB // 512)
+        @pl.loop(0, HB // 512)
         def _(n):
             cols = pl.ds(pl.multiple_of(n * 512, 512), 512)
-            dcols = pl.ds(pl.multiple_of(DA + n * 512, 512), 512)
+            dcols = pl.ds(pl.multiple_of(HA + n * 512, 512), 512)
             y = jnp.dot(actp, dw[:, dcols], preferred_element_type=F32)
             yB[g, :, :, cols] = y.reshape(16, 8, 512).astype(BF)
 
@@ -567,7 +549,7 @@
             home.append(cp)
         rB[g, e] = yB[g, e]
 
-        @pl.loop(0, DA // 512)
+        @pl.loop(0, HA // 512)
         def _(n):
             cols = pl.ds(pl.multiple_of(n * 512, 512), 512)
             y = jnp.dot(act, dw[:, cols], preferred_element_type=F32).astype(BF)
@@ -618,7 +600,7 @@
     def gather_home(g):
         for j in range(1, 16):
             rcopy(yB.at[g, 0], rB.at[g, 0], sy.at[g, j], qy.at[g, j], sib).wait_recv()
-        x = rB[g].astype(F32).reshape(128, DB).astype(BF)
+        x = rB[g].astype(F32).reshape(128, HB).astype(BF)
         y = jnp.dot(weigh_b[g], x, preferred_element_type=F32)
         y = y[0:32] + y[32:64] + y[64:96]
         for i, r in enumerate(NEAR[g]):
@@ -640,9 +622,9 @@
             n = 5 + (chunk if way == 0 else 1 - chunk)
             leg(way, n, rv.at[way, n]).wait_recv()
             total = total + rv[way, n].astype(F32)
-        fs[16 * chunk : 16 * chunk + 16] = total
+        fs[16 * chunk : 16 * chunk + 16, :HA] = total
     for i in range(16):
-        ro[i] = fs[2 * i : 2 * i + 2, :].astype(BF)
+        ro[i] = fs[2 * i : 2 * i + 2, :HA].astype(BF)
     last = []
     for j in range(1, 16):
         cp = rcopy(ro.at[lax.rem(e + j, 16)], ra.at[e], sh.at[j], qh.at[j], plane[j - 1])
@@ -653,77 +635,95 @@
     for cp in last:
         cp.wait_recv()
     for i in range(16):
-        fs[2 * i : 2 * i + 2, :] = ra[i].astype(F32)
-    y = jnp.dot(weigh_a, fs[...].astype(BF), preferred_element_type=F32)
-    out[:, :DA] = (hs[:, :DA] + (y[0:8] + y[8:16] + y[16:24])).astype(BF)
-    total = hs[:, DA:] + zs[0].astype(F32)
+        fs[2 * i : 2 * i + 2, :HA] = ra[i].astype(F32)
+    y = jnp.dot(weigh_a, fs[:, :HA].astype(BF), preferred_element_type=F32)
+    out[:, :HA] = (hs[:, :HA] + (y[0:8] + y[8:16] + y[16:24])).astype(BF)
+    total = hs[:, HA:] + zs[0].astype(F32)
     for r in range(1, 8):
         rcopy(zs.at[0], zr.at[r], sz.at[0], qz.at[r], sib).wait_recv()
         total = total + zr[r].astype(F32)
-    out[:, DA:] = total.astype(BF)
-
+    out[:, HA:] = total.astype(BF)
+
+    drain()
     for r in wide + thin:
         r[3]()
     for cp in sent + share + told + moved + spoke + go + sent2 + home + back + part + last:
         cp.wait_send()
 
 
-def run_tail(att, wp, res, gain, ids, gts, eg, eu, ed):
+def run(q, k, v, g, cw, wo, res, gain, ids, gts, eg, eu, ed):
     vm = pl.BlockSpec(memory_space=pltpu.VMEM)
     hbm = pl.BlockSpec(memory_space=pltpu.HBM)
 
     def dma(*shape):
         return pltpu.SemaphoreType.DMA(shape)
+
+    def bf(*shape):
+        return pltpu.VMEM(shape, BF)
+
+    def f32(*shape):
+        return pltpu.VMEM(shape, F32)
 
     return pl.pallas_call(
         tail,
         out_shape=jax.ShapeDtypeStruct((8, 7168), BF),
-        in_specs=[vm] * 6 + [hbm] * 3,
+        in_specs=[hbm] * 3 + [vm] * 2 + [hbm] + [vm] * 4 + [hbm] * 3,
         out_specs=vm,
         scratch_shapes=[
-            pltpu.VMEM((128, 128), F32),
-            pltpu.VMEM((8, 8, 128), F32),
-            pltpu.VMEM((8, 7168), F32),
-            pltpu.VMEM((8, 8, 896), BF),
-            pltpu.VMEM((8, 2, 128, 256), BF),
-            pltpu.VMEM((8, 4, 4, 8, 896), BF),
-            pltpu.VMEM((2, 2, 2, 4, 8, 896), BF),
-            pltpu.VMEM((2, 2, 4, 4, 8, 896), BF),
-            pltpu.VMEM((2, 2, 2, 4, 8, 896), BF),
-            pltpu.VMEM((2, 4, 4, 8, 896), BF),
-            pltpu.VMEM((2, 2, 2, 8, 896), BF),
-            pltpu.VMEM((2, 2, 4, 8, 896), BF),
-            pltpu.VMEM((2, 2, 2, 8, 896), BF),
-            pltpu.VMEM((8, 8, 896), BF),
+            bf(896, 512),
+            bf(3, 2, 128, 256),
+            bf(3, 2, 128, 256),
+            bf(2, 128, 256),
+            f32(2, 2, 4, 128),
+            f32(2, 128, 128),
+            bf(16, 256),
+            bf(16, 256),
+            bf(8, 2, 16, 256),
+            bf(2, 128, 256),
+            dma(29), dma(29), dma(4),
+            f32(128, 128),
+            f32(8, 8, 128),
+            f32(8, 7168),
+            bf(8, 8, 896),
+            bf(8, 2, 128, 256),
+            bf(8, 4, 4, 8, 896),
+            bf(2, 2, 2, 4, 8, 896),
+            bf(2, 2, 4, 4, 8, 896),
+            bf(2, 2, 2, 4, 8, 896),
+            bf(2, 4, 4, 8, 896),
+            bf(2, 2, 2, 8, 896),
+            bf(2, 2, 4, 8, 896),
+            bf(2, 2, 2, 8, 896),
+            bf(8, 8, 896),
             dma(14), dma(14), dma(12), dma(12), dma(12), dma(12), dma(8), dma(8), dma(8), dma(8),
-            pltpu.VMEM((7168, 512), BF),
-            pltpu.VMEM((256, 7168), BF),
+            bf(7168, 512),
+            bf(256, 7168),
             dma(3), dma(3), dma(3),
-            pltpu.VMEM((16, 2, DA), BF),
-            pltpu.VMEM((16, 2, DA), BF),
-            pltpu.VMEM((8, 2, 16, DA), BF),
-            pltpu.VMEM((8, 2, 16, DA), BF),
-            pltpu.VMEM((2, 7, 16, DA), BF),
-            pltpu.VMEM((2, 7, 16, DA), BF),
-            pltpu.VMEM((32, DA), F32),
-            pltpu.VMEM((16, 2, DA), BF),
-            pltpu.VMEM((16, 2, DA), BF),
-            pltpu.VMEM((8, DB), BF),
-            pltpu.VMEM((8, 8, DB), BF),
-            pltpu.VMEM((2, 16, 8, DB), BF),
-            pltpu.VMEM((2, 16, 8, DB), BF),
-            pltpu.VMEM((2, 16, 8, DB), BF),
-            pltpu.VMEM((2, 16, 8, DB), BF),
-            pltpu.VMEM((8, 8, DB), BF),
-            pltpu.VMEM((8, 8, DB), BF),
+            bf(16, 2, DA),
+            bf(16, 2, DA),
+            bf(8, 2, 16, DA),
+            bf(8, 2, 16, HA),
+            bf(2, 7, 16, HA),
+            bf(2, 7, 16, HA),
+            f32(32, max(DA, HA)),
+            bf(16, 2, HA),
+            bf(16, 2, HA),
+            bf(8, DB),
+            bf(8, 8, DB),
+            bf(2, 16, 8, DB),
+            bf(2, 16, 8, DB),
+            bf(2, 16, 8, HB),
+            bf(2, 16, 8, HB),
+            bf(8, 8, HB),
+            bf(8, 8, HB),
             dma(16), dma(16), dma(2, 16), dma(2, 16), dma(8), dma(8), dma(14), dma(14),
             dma(2, 16), dma(2, 16), dma(14), dma(14), dma(16), dma(16), dma(8), dma(8),
         ],
         compiler_params=pltpu.CompilerParams(
             collective_id=2, has_side_effects=True, vmem_limit_bytes=67043328
         ),
-        name="tail",
-    )(att, wp, res, gain, ids, gts, eg, eu, ed)
+        name="layer",
+    )(q, k, v, g, cw, wo, res, gain, ids, gts, eg, eu, ed)
 
 
 def local(
@@ -742,10 +742,9 @@
     expert_down,
 ):
     gates = gate_logits.transpose(0, 2, 1)
-    cw = jnp.broadcast_to(comp_weight.transpose(0, 2, 1)[..., None], (2, 4, 32, 128))
-    att, wpair = run_attention(query_input, key_input, value_input, gates, cw, out_proj.T)
-    return run_tail(
-        att, wpair, residual_in, ffn_gain.reshape(1, 7168), expert_ids.T, route_gates.T,
+    return run(
+        query_input, key_input, value_input, gates, comp_weight.transpose(0, 2, 1), out_proj.T,
+        residual_in, ffn_gain.reshape(1, 7168), expert_ids.T, route_gates.T,
         expert_gate[0], expert_up[0], expert_down[0],
     )
 

time: 151 us -> 143 us (0.947)
  Pallas kernels: 146 us -> 140 us
    pallas_call x2 -> x1, Pallas kernels: 146 us -> 140 us  [run(): pl.pallas_call(tail, out_shape=jax.ShapeDtypeStruct((8, 7168), BF), in_sp...]
where the time goes in v3:
time: 143 us; the launch traced here: 141 us
  Pallas kernels  140 us (98%)
  local copies, waits for them, and re-layouts  1.55 us (1%)
    pallas_call x1, Pallas kernels, run(): pl.pallas_call(tail, out_shape=jax.ShapeDtypeStruct((8, 7168), BF), in_sp...  140 us

profile of v3, /device:TPU:32, one launch (start us, length us, event | category | flops | bytes accessed | tf_op | source)
XLA Modules:
  0.0 141.3 jit_solution(11020215462780164981)
XLA Ops:
  0.0 139.7 %layer.1 = bf16[8,7168]{1,0:T(8,128)(2,1)} custom-call(bf16[128,512]{1,0:T(8,128)(2,1)} %q.1, bf16[128,512]{1,0:T(8,128)(2,1)} %k.1, bf16[128,512]{1,0:T(8,128)(2,1)} %v.1, f32[2,4,128]{2,1,0:T(4,128)} %bitcast.14, f32[2,4,32]{2,1,0:T(4,128)} %bitcast.15, bf16[448,512]{1,0:T(8,128)(2,1)} %bitcast.12, bf16[8,7168]{1,0:T(8,128)(2,1)} %res.1, ...), custom_call_target="tpu_custom_call" | custom-call | tf_op jit(solution)/shard_map/layer/pallas_call | solution.py:667
  139.7 1.6 %copy.15 = bf16[8,7168]{1,0:T(8,128)(2,1)} copy(bf16[8,7168]{1,0:T(8,128)(2,1)} %layer.1) | data formatting | bytes 229376

commit v4 on v3

--- a/solution.py
+++ b/solution.py
@@ -46,8 +46,8 @@
     off_other = pl.multiple_of(other * 256, 256)
     off = pl.multiple_of(core * 256, 256)
     near = []
-    for kk in range(2):
-        for a, (src, dst) in enumerate(((k, kb), (v, vb))):
+    for a, (src, dst) in enumerate(((k, kb), (v, vb))):
+        for kk in range(2):
             near.append(
                 rcopy(
                     src.at[:, pl.ds(kk * 256, 256)],
@@ -104,8 +104,8 @@
 
     relay = []
 
-    def pass_on(n):
-        for a, buf in enumerate((kb, vb)):
+    def pass_on(a, buf):
+        for n in range(2):
             rcopy(buf.at[1, n], buf.at[1, n], ss.at[8], rs.at[8 + 2 * n + a], sib).wait_recv()
             cp = rcopy(
                 buf.at[1, n],
@@ -144,19 +144,19 @@
 
     for cp in own:
         cp.wait()
-    pass_on(0)
     for cp in swap:
         cp.wait_recv()
     for cp in halo[:2]:
         cp.wait_recv()
     squeeze(0, kb, hk)
-    pass_on(1)
     squeeze(1, vb, hv)
     comps = [
         rcopy(cb.at[z], cb.at[z], ss.at[20 + j], rs.at[20 + j], peers[j - 1]) for j in range(1, 8)
     ]
     for cp in comps:
         cp.start()
+    pass_on(0, kb)
+    pass_on(1, vb)
     for cp in comps:
         cp.wait_recv()
     for cp in relay:
@@ -225,16 +225,17 @@
     return copy, chunks
 
 
-def gather_start(copy, chunk, sent):
+def gather_start(copy, chunk, sent, flip=0):
     for way in (0, 1):
-        cp = copy(way, 0, chunk)
+        cp = copy(way, 0, (chunk + way * flip) % 2)
         cp.start()
         sent.append(cp)
 
 
-def gather_step(copy, chunks, step, sent):
-    for chunk in (0, 1):
+def gather_step(copy, chunks, step, sent, flip=0):
+    for n in (0, 1):
         for way in (0, 1):
+            chunk = (n + way * flip) % 2
             if chunk in chunks(way, step):
                 copy(way, step, chunk).wait_recv()
                 if step < 3 and chunk in chunks(way, step + 1):
@@ -272,8 +273,8 @@
     out,
     wp, kb, vb, qb, gb, gs, hk, hv, cb, tb, s0, r0, l0,
     sc, inf, hs, hid,
-    xb, pb, a1, a2, a3, sb, c1, c2, c3, rb, ss, rs, s1, r1, s2, r2, s3, r3, si, ri,
-    gw, dw, sw, rw, ls,
+    xb, pb, a1, a2, a3, sb, c2, rb, ss, rs, s1, r1, s2, r2, s3, r3, si, ri,
+    gw, dw, ys, sw, rw, ls,
     oa, aa, xa, ya, rv, mx, fs, ro, ra, tk, tr, sB, aB, yB, rB, zs, zr,
     sa, qa, sg, qg, st, qt, sx, qx, sy, qy, sv, qv, sh, qh, sz, qz,
 ):
@@ -344,25 +345,23 @@
     swapped.wait_recv()
     gather_start(copy, 1, sent)
     outw.wait_recv()
-    partial(z, 0)
-    for step in range(4):
-        gather_step(copy, chunks, step, sent)
-        partial(lax.rem(z + step + 1, 8), step + 1)
-        if step < 3:
-            partial(lax.rem(z + 7 - step, 8), 7 - step)
-
-    def ring_sum(which, half, piece, first, second, mixed, ssem, rsem):
+
+    def ring_sum(which, g, half, piece, first, second, mixed, ssem, rsem):
         p, dev = ring[which]
         nxt, prv = dev(p + 1), dev(p + 3)
-        base = 6 * half
+        base = 12 * g + 6 * half
         far, nt, pt = lax.rem(p + 2, 4), lax.rem(p + 1, 4), lax.rem(p + 3, 4)
+        legs = [
+            (piece(far, 0), first.at[g, half, 0], nxt),
+            (piece(far, 1), first.at[g, half, 1], prv),
+            (piece(nt, 1), second.at[g, half, 0, 1], nxt),
+            (piece(pt, 0), second.at[g, half, 1, 0], prv),
+            (mixed.at[g, half, 0], second.at[g, half, 0, 0], nxt),
+            (mixed.at[g, half, 1], second.at[g, half, 1, 1], prv),
+        ]
         cps = [
-            rcopy(piece(far, 0), first.at[half, 0], ssem.at[base], rsem.at[base], nxt),
-            rcopy(piece(far, 1), first.at[half, 1], ssem.at[base + 1], rsem.at[base + 1], prv),
-            rcopy(piece(nt, 1), second.at[half, 0, pl.ds(2, 2)], ssem.at[base + 2], rsem.at[base + 2], nxt),
-            rcopy(piece(pt, 0), second.at[half, 1, pl.ds(0, 2)], ssem.at[base + 3], rsem.at[base + 3], prv),
-            rcopy(mixed.at[half, 0], second.at[half, 0, pl.ds(0, 2)], ssem.at[base + 4], rsem.at[base + 4], nxt),
-            rcopy(mixed.at[half, 1], second.at[half, 1, pl.ds(2, 2)], ssem.at[base + 5], rsem.at[base + 5], prv),
+            rcopy(src, dst, ssem.at[base + n], rsem.at[base + n], dev)
+            for n, (src, dst, dev) in enumerate(legs)
         ]
 
         def start():
@@ -370,20 +369,20 @@
                 cp.start()
 
         def middle():
-            cps[0].wait_recv()
-            mixed[half, 0] = (first[half, 0].astype(F32) + piece(nt, 0)[...].astype(F32)).astype(BF)
-            cps[4].start()
-            cps[1].wait_recv()
-            mixed[half, 1] = (first[half, 1].astype(F32) + piece(pt, 1)[...].astype(F32)).astype(BF)
-            cps[5].start()
+            for n, t in ((0, nt), (1, pt)):
+                cps[n].wait_recv()
+                mixed[g, half, n] = (
+                    first[g, half, n].astype(F32) + piece(t, n)[...].astype(F32)
+                ).astype(BF)
+                cps[4 + n].start()
 
         def end():
             for cp in cps[2:]:
                 cp.wait_recv()
             return [
                 piece(p, n)[...].astype(F32)
-                + second[half, 0, 2 * n : 2 * n + 2].astype(F32)
-                + second[half, 1, 2 * n : 2 * n + 2].astype(F32)
+                + second[g, half, 0, n].astype(F32)
+                + second[g, half, 1, n].astype(F32)
                 for n in range(2)
             ]
 
@@ -393,45 +392,85 @@
 
         return start, middle, end, drain
 
-    def piece_a(t, n):
-        return pb.at[pl.ds(2 * n, 2), t]
-
-    def piece_b(t, n):
-        return pb.at[pl.ds(4 + 2 * n, 2), :, t]
-
-    def piece_of(half):
-        return lambda t, n: sb.at[half, pl.ds(2 * n, 2), t]
+    def piece_a(g):
+        return lambda t, n: pb.at[4 * g + n, t]
+
+    def piece_b(g):
+        return lambda t, n: pb.at[4 * g + 2 + n, :, t]
 
     wide = [
-        ring_sum(0, 0, piece_a, a1, a2, a3, s1, r1),
-        ring_sum(1, 1, piece_b, a1, a2, a3, s1, r1),
+        [
+            ring_sum(0, g, 0, piece_a(g), a1, a2, a3, s1, r1),
+            ring_sum(1, g, 1, piece_b(g), a1, a2, a3, s1, r1),
+        ]
+        for g in range(2)
     ]
-    thin = [
-        ring_sum(1, 0, piece_of(0), c1, c2, c3, s2, r2),
-        ring_sum(0, 1, piece_of(1), c1, c2, c3, s2, r2),
-    ]
-    for r in wide:
-        r[0]()
-    for r in wide:
-        r[1]()
-    for half in range(2):
-        lo, hi = wide[half][2]()
-        sb[half, 0:2] = lo.astype(BF)
-        sb[half, 2:4] = hi.astype(BF)
-        thin[half][0]()
-    for r in thin:
-        r[1]()
+    thin = []
     moved = []
-    for half in range(2):
-        lo, hi = thin[half][2]()
-        rb[4 * half : 4 * half + 2] = lo.astype(BF)
-        rb[4 * half + 2 : 4 * half + 4] = hi.astype(BF)
-        for j in range(4 * half, 4 * half + 4):
-            if j:
-                cp = rcopy(rb.at[j], hid.at[z], s3.at[j], r3.at[j], zp[j - 1])
+
+    def fan(g, stage):
+        for r in wide[g]:
+            r[stage]()
+
+    def turn(g):
+        for half in range(2):
+            for n, y in enumerate(wide[g][half][2]()):
+                sb[g, half, :, n] = y.astype(BF)
+            p, dev = ring[1 - half]
+            for j in (2, 1, 3):
+                n = 4 * (2 * g + half) + j
+                cp = rcopy(
+                    sb.at[g, half, lax.rem(p + j, 4)], c2.at[g, half, j], s2.at[n], r2.at[n], dev(p + j)
+                )
                 cp.start()
-                moved.append(cp)
-    hid[z] = rb[0]
+                thin.append(cp)
+
+    def move(g):
+        for half in range(2):
+            for cp in thin[6 * g + 3 * half : 6 * g + 3 * half + 3]:
+                cp.wait_recv()
+            total = sb[g, half, ring[1 - half][0]].astype(F32)
+            for j in range(1, 4):
+                total = total + c2[g, half, j].astype(F32)
+            for n in range(2):
+                r = NEAR[g][2 * half + n]
+                rb[r] = total[n].astype(BF)
+                if r:
+                    cp = rcopy(rb.at[r], hid.at[z], s3.at[r], r3.at[r], zp[r - 1])
+                    cp.start()
+                    moved.append(cp)
+                else:
+                    hid[z] = rb[0]
+
+    def partial(place):
+        r = NEAR[place // 4][place % 4]
+        block = lax.rem(z + r, 8)
+        x0, x1 = xb[block, 0], xb[block, 1]
+        dims = (((1,), (1,)), ((), ()))
+        y = lax.dot_general(x0, wp[:, :256], dims, preferred_element_type=F32)
+        y = y + lax.dot_general(x1, wp[:, 256:], dims, preferred_element_type=F32)
+        pb[place] = y.reshape(4, 4, 8, 896).astype(BF)
+
+    partial(0)
+    gather_step(copy, chunks, 0, sent)
+    partial(1)
+    partial(2)
+    gather_step(copy, chunks, 1, sent)
+    partial(3)
+    fan(0, 0)
+    partial(4)
+    gather_step(copy, chunks, 2, sent)
+    fan(0, 1)
+    partial(5)
+    partial(6)
+    turn(0)
+    gather_step(copy, chunks, 3, sent)
+    partial(7)
+    fan(1, 0)
+    move(0)
+    fan(1, 1)
+    turn(1)
+    move(1)
 
     for cp in told:
         cp.wait_recv()
@@ -511,8 +550,8 @@
     xa[z, 1] = fs[16:32, :DA].astype(BF)
     copy2, chunks2 = z_ring(xa, z, core, e, sx, qx, 0)
     sent2 = []
-    gather_start(copy2, 0, sent2)
-    gather_start(copy2, 1, sent2)
+    gather_start(copy2, 0, sent2, 1)
+    gather_start(copy2, 1, sent2, 1)
     scatter(1)
     for cp in load:
         cp.wait()
@@ -521,15 +560,17 @@
 
     home = []
 
-    def work(g):
-        blocks = [lax.rem(z + r, 8) for r in NEAR[g]]
-        x = jnp.concatenate([xa[b, n] for b in blocks for n in range(2)], 0)
-        y = jnp.dot(x, gw[0:DA, :], preferred_element_type=F32)
+    def early(g):
         for j in range(1, 16):
             rcopy(sB.at[g, 0], aB.at[g, 0], sg.at[g, j], qg.at[g, j], sib).wait_recv()
         x = aB[g].astype(F32).reshape(128, DB).astype(BF)
         x = jnp.dot(order, x, preferred_element_type=F32).astype(BF)
-        y = y + jnp.dot(x, gw[DA:, :], preferred_element_type=F32)
+        ys[...] = jnp.dot(x, gw[DA:, :], preferred_element_type=F32)
+
+    def work(g):
+        blocks = [lax.rem(z + r, 8) for r in NEAR[g]]
+        x = jnp.concatenate([xa[b, n] for b in blocks for n in range(2)], 0)
+        y = jnp.dot(x, gw[0:DA, :], preferred_element_type=F32) + ys[...]
         gate, lift = y[:, :256], y[:, 256:]
         act = (gate / (1.0 + jnp.exp(-gate)) * lift).astype(BF)
         actp = jnp.dot(unorder, act, preferred_element_type=F32).astype(BF)
@@ -557,11 +598,13 @@
                 ya[b, 0, :, cols] = y[32 * i : 32 * i + 16]
                 ya[b, 1, :, cols] = y[32 * i + 16 : 32 * i + 32]
 
-    gather_step(copy2, chunks2, 0, sent2)
-    gather_step(copy2, chunks2, 1, sent2)
+    gather_step(copy2, chunks2, 0, sent2, 1)
+    gather_step(copy2, chunks2, 1, sent2, 1)
+    early(0)
     work(0)
-    gather_step(copy2, chunks2, 2, sent2)
-    gather_step(copy2, chunks2, 3, sent2)
+    gather_step(copy2, chunks2, 2, sent2, 1)
+    early(1)
+    gather_step(copy2, chunks2, 3, sent2, 1)
     work(1)
 
     up, down = zp[0], zp[6]
@@ -611,11 +654,11 @@
                 part.append(cp)
 
     along(1, 3, 0, 0)
+    along(4, 2, 1, 2)
     along(3, 2, 0, 1)
-    along(4, 2, 1, 2)
     gather_home(0)
+    along(6, 1, 1, 4)
     along(5, 1, 0, 3)
-    along(6, 1, 1, 4)
     for chunk in range(2):
         total = ya[z, chunk].astype(F32)
         for way in (0, 1):
@@ -645,9 +688,9 @@
     out[:, HA:] = total.astype(BF)
 
     drain()
-    for r in wide + thin:
+    for r in wide[0] + wide[1]:
         r[3]()
-    for cp in sent + share + told + moved + spoke + go + sent2 + home + back + part + last:
+    for cp in sent + share + told + thin + moved + spoke + go + sent2 + home + back + part + last:
         cp.wait_send()
 
 
@@ -688,16 +731,15 @@
             bf(8, 2, 128, 256),
             bf(8, 4, 4, 8, 896),
             bf(2, 2, 2, 4, 8, 896),
-            bf(2, 2, 4, 4, 8, 896),
+            bf(2, 2, 2, 2, 4, 8, 896),
             bf(2, 2, 2, 4, 8, 896),
-            bf(2, 4, 4, 8, 896),
-            bf(2, 2, 2, 8, 896),
-            bf(2, 2, 4, 8, 896),
-            bf(2, 2, 2, 8, 896),
+            bf(2, 2, 4, 2, 8, 896),
+            bf(2, 2, 4, 2, 8, 896),
             bf(8, 8, 896),
-            dma(14), dma(14), dma(12), dma(12), dma(12), dma(12), dma(8), dma(8), dma(8), dma(8),
+            dma(14), dma(14), dma(24), dma(24), dma(16), dma(16), dma(8), dma(8), dma(8), dma(8),
             bf(7168, 512),
             bf(256, 7168),
+            f32(128, 512),
             dma(3), dma(3), dma(3),
             bf(16, 2, DA),
             bf(16, 2, DA),

time: 143 us -> 138 us (0.965)
  Pallas kernels: 140 us -> 134 us
    pallas_call x1, Pallas kernels: 140 us -> 134 us  [run(): pl.pallas_call(tail, out_shape=jax.ShapeDtypeStruct((8, 7168), BF), in_sp...]
where the time goes in v4:
time: 138 us; the launch traced here: 136 us
  Pallas kernels  134 us (97%)
  local copies, waits for them, and re-layouts  1.55 us (1%)
    pallas_call x1, Pallas kernels, run(): pl.pallas_call(tail, out_shape=jax.ShapeDtypeStruct((8, 7168), BF), in_sp...  134 us

profile of v4, /device:TPU:32, one launch (start us, length us, event | category | flops | bytes accessed | tf_op | source)
XLA Modules:
  0.0 135.8 jit_solution(6887587707053039751)
XLA Ops:
  0.0 134.3 %layer.1 = bf16[8,7168]{1,0:T(8,128)(2,1)} custom-call(bf16[128,512]{1,0:T(8,128)(2,1)} %q.1, bf16[128,512]{1,0:T(8,128)(2,1)} %k.1, bf16[128,512]{1,0:T(8,128)(2,1)} %v.1, f32[2,4,128]{2,1,0:T(4,128)} %bitcast.14, f32[2,4,32]{2,1,0:T(4,128)} %bitcast.15, bf16[448,512]{1,0:T(8,128)(2,1)} %bitcast.12, bf16[8,7168]{1,0:T(8,128)(2,1)} %res.1, ...), custom_call_target="tpu_custom_call" | custom-call | tf_op jit(solution)/shard_map/layer/pallas_call | solution.py:710
  134.3 1.6 %copy.15 = bf16[8,7168]{1,0:T(8,128)(2,1)} copy(bf16[8,7168]{1,0:T(8,128)(2,1)} %layer.1) | data formatting | bytes 229376

commit v5 on v4

--- a/solution.py
+++ b/solution.py
@@ -151,7 +151,8 @@
     squeeze(0, kb, hk)
     squeeze(1, vb, hv)
     comps = [
-        rcopy(cb.at[z], cb.at[z], ss.at[20 + j], rs.at[20 + j], peers[j - 1]) for j in range(1, 8)
+        rcopy(cb.at[z], cb.at[z], ss.at[20 + j], rs.at[20 + j], peers[j - 1])
+        for j in (4, 3, 5, 2, 6, 1, 7)
     ]
     for cp in comps:
         cp.start()
@@ -244,10 +245,14 @@
                     sent.append(cp)
 
 
-DA = 4096
+DA = 4352
 DB = 7168 - DA
 HA = 3584
 HB = 7168 - HA
+FAR = (
+    (2, 2), (2, 1), (1, 2), (2, 3), (3, 2), (1, 1), (3, 3), (1, 3), (3, 1), (2, 0), (0, 2),
+    (1, 0), (0, 1), (3, 0), (0, 3),
+)
 NEAR = ((0, 1, 7, 2), (6, 3, 5, 4))
 
 
@@ -275,7 +280,7 @@
     sc, inf, hs, hid,
     xb, pb, a1, a2, a3, sb, c2, rb, ss, rs, s1, r1, s2, r2, s3, r3, si, ri,
     gw, dw, ys, sw, rw, ls,
-    oa, aa, xa, ya, rv, mx, fs, ro, ra, tk, tr, sB, aB, yB, rB, zs, zr,
+    oa, aa, xa, ya, rv, mx, fs, ro, ra, tr, sB, aB, yB, rB, zs, zr,
     sa, qa, sg, qg, st, qt, sx, qx, sy, qy, sv, qv, sh, qh, sz, qz,
 ):
     z, core, e = place()
@@ -287,7 +292,8 @@
         (ey, lambda t: (c, 4 * ex + lax.rem(t, 4))),
     ]
     zp = [(2 * lax.rem(z + j, 8) + core, e) for j in range(1, 8)]
-    plane = [(c, lax.rem(e + j, 16)) for j in range(1, 16)]
+    dest = [4 * lax.rem(ex + a, 4) + lax.rem(ey + b, 4) for a, b in FAR]
+    plane = [(c, d) for d in dest]
     cross = [(2 * lax.rem(z + j, 8) + 1 - core, e) for j in (1, 7)]
     greet(plane + zp + [sib] + cross)
     outw, swapped, drain = attend(
@@ -504,13 +510,20 @@
     h = hs[...]
     normed = h * lax.rsqrt(jnp.mean(h * h, axis=1, keepdims=True) + EPS) * gain[...]
 
-    tk[...] = normed[:, DA:].astype(BF)
-    tr[0] = tk[...]
+    tr[0] = normed[:, DA:].astype(BF)
     spoke = []
-    for j in (1, 7, 2, 6, 3, 5, 4):
-        cp = rcopy(tk, tr.at[8 - j], st.at[j], qt.at[8 - j], zp[j - 1])
+
+    def tell(r):
+        src, dev = (tr.at[r - 1], zp[6]) if r <= 4 else (tr.at[(r + 1) % 8], zp[0])
+        cp = rcopy(src, tr.at[r], st.at[r], qt.at[r], dev)
         cp.start()
         spoke.append(cp)
+
+    def heard(r):
+        rcopy(tr.at[0], tr.at[r], st.at[0], qt.at[r], sib).wait_recv()
+
+    tell(1)
+    tell(7)
 
     padded = jnp.concatenate([normed[:, :DA], jnp.zeros((8, DA), F32)], 0).astype(BF)
     fs[:, :DA] = jnp.dot(spread_a, padded, preferred_element_type=F32)
@@ -518,29 +531,31 @@
         oa[i] = fs[2 * i : 2 * i + 2, :DA].astype(BF)
     go = []
     for j in range(1, 16):
-        cp = rcopy(oa.at[lax.rem(e + j, 16)], aa.at[e], sa.at[j], qa.at[j], plane[j - 1])
+        cp = rcopy(oa.at[dest[j - 1]], aa.at[e], sa.at[j], qa.at[j], plane[j - 1])
         cp.start()
         go.append(cp)
     aa[e] = oa[e]
 
-    def heard(r):
-        rcopy(tk, tr.at[r], st.at[0], qt.at[r], sib).wait_recv()
-
     def scatter(g):
-        for r in NEAR[g]:
-            if r:
-                heard(r)
         x = jnp.concatenate([tr[r].astype(F32) for r in NEAR[g]], 0).astype(BF)
         y = jnp.dot(spread_b[g], x, preferred_element_type=F32)
         sB[g] = y.reshape(16, 8, DB).astype(BF)
         for j in range(1, 16):
             cp = rcopy(
-                sB.at[g, lax.rem(e + j, 16)], aB.at[g, e], sg.at[g, j], qg.at[g, j], plane[j - 1]
+                sB.at[g, dest[j - 1]], aB.at[g, e], sg.at[g, j], qg.at[g, j], plane[j - 1]
             )
             cp.start()
             go.append(cp)
         aB[g, e] = sB[g, e]
 
+    heard(1)
+    tell(2)
+    heard(7)
+    tell(6)
+    heard(2)
+    tell(3)
+    heard(6)
+    tell(5)
     scatter(0)
     for cp in go[:15]:
         cp.wait_recv()
@@ -552,11 +567,13 @@
     sent2 = []
     gather_start(copy2, 0, sent2, 1)
     gather_start(copy2, 1, sent2, 1)
-    scatter(1)
     for cp in load:
         cp.wait()
     for cp in share:
         cp.wait_recv()
+    heard(3)
+    tell(4)
+    heard(5)
 
     home = []
 
@@ -584,7 +601,7 @@
 
         for j in range(1, 16):
             cp = rcopy(
-                yB.at[g, lax.rem(e + j, 16)], rB.at[g, e], sy.at[g, j], qy.at[g, j], plane[j - 1]
+                yB.at[g, dest[j - 1]], rB.at[g, e], sy.at[g, j], qy.at[g, j], plane[j - 1]
             )
             cp.start()
             home.append(cp)
@@ -599,6 +616,8 @@
                 ya[b, 1, :, cols] = y[32 * i + 16 : 32 * i + 32]
 
     gather_step(copy2, chunks2, 0, sent2, 1)
+    heard(4)
+    scatter(1)
     gather_step(copy2, chunks2, 1, sent2, 1)
     early(0)
     work(0)
@@ -659,6 +678,7 @@
     gather_home(0)
     along(6, 1, 1, 4)
     along(5, 1, 0, 3)
+    gather_home(1)
     for chunk in range(2):
         total = ya[z, chunk].astype(F32)
         for way in (0, 1):
@@ -670,11 +690,10 @@
         ro[i] = fs[2 * i : 2 * i + 2, :HA].astype(BF)
     last = []
     for j in range(1, 16):
-        cp = rcopy(ro.at[lax.rem(e + j, 16)], ra.at[e], sh.at[j], qh.at[j], plane[j - 1])
+        cp = rcopy(ro.at[dest[j - 1]], ra.at[e], sh.at[j], qh.at[j], plane[j - 1])
         cp.start()
         last.append(cp)
     ra[e] = ro[e]
-    gather_home(1)
     for cp in last:
         cp.wait_recv()
     for i in range(16):
@@ -750,7 +769,6 @@
             f32(32, max(DA, HA)),
             bf(16, 2, HA),
             bf(16, 2, HA),
-            bf(8, DB),
             bf(8, 8, DB),
             bf(2, 16, 8, DB),
             bf(2, 16, 8, DB),

time: 138 us -> 132 us (0.957); the launches traced: 136 us -> 132 us
  Pallas kernels: 134 us -> 131 us
    pallas_call x1, Pallas kernels: 134 us -> 131 us  [run(): pl.pallas_call(tail, out_shape=jax.ShapeDtypeStruct((8, 7168), BF), in_sp...]
where the time goes in v5:
time: 132 us
  Pallas kernels  131 us (99%)
  local copies, waits for them, and re-layouts  1.55 us (1%)
    pallas_call x1, Pallas kernels, run(): pl.pallas_call(tail, out_shape=jax.ShapeDtypeStruct((8, 7168), BF), in_sp...  131 us

profile of v5, /device:TPU:32, one launch (start us, length us, event | category | flops | bytes accessed | tf_op | source)
XLA Modules:
  0.0 132.2 jit_solution(7800699804860001614)
XLA Ops:
  0.0 130.7 %layer.1 = bf16[8,7168]{1,0:T(8,128)(2,1)} custom-call(bf16[128,512]{1,0:T(8,128)(2,1)} %q.1, bf16[128,512]{1,0:T(8,128)(2,1)} %k.1, bf16[128,512]{1,0:T(8,128)(2,1)} %v.1, f32[2,4,128]{2,1,0:T(4,128)} %bitcast.14, f32[2,4,32]{2,1,0:T(4,128)} %bitcast.15, bf16[448,512]{1,0:T(8,128)(2,1)} %bitcast.12, bf16[8,7168]{1,0:T(8,128)(2,1)} %res.1, ...), custom_call_target="tpu_custom_call" | custom-call | tf_op jit(solution)/shard_map/layer/pallas_call | solution.py:729
  130.7 1.6 %copy.15 = bf16[8,7168]{1,0:T(8,128)(2,1)} copy(bf16[8,7168]{1,0:T(8,128)(2,1)} %layer.1) | data formatting | bytes 229376

commit v6 on v5

--- a/solution.py
+++ b/solution.py
@@ -245,7 +245,7 @@
                     sent.append(cp)
 
 
-DA = 4352
+DA = 4608
 DB = 7168 - DA
 HA = 3584
 HB = 7168 - HA

time: 132 us -> 131 us (level)
  Pallas kernels: 131 us -> 129 us
    pallas_call x1, Pallas kernels: 131 us -> 129 us  [run(): pl.pallas_call(tail, out_shape=jax.ShapeDtypeStruct((8, 7168), BF), in_sp...]
where the time goes in v6:
time: 131 us; the launch traced here: 130 us
  Pallas kernels  129 us (98%)
  local copies, waits for them, and re-layouts  1.55 us (1%)
    pallas_call x1, Pallas kernels, run(): pl.pallas_call(tail, out_shape=jax.ShapeDtypeStruct((8, 7168), BF), in_sp...  129 us

profile of v6, /device:TPU:32, one launch (start us, length us, event | category | flops | bytes accessed | tf_op | source)
XLA Modules:
  0.0 130.1 jit_solution(757351314596281521)
XLA Ops:
  0.0 128.5 %layer.1 = bf16[8,7168]{1,0:T(8,128)(2,1)} custom-call(bf16[128,512]{1,0:T(8,128)(2,1)} %q.1, bf16[128,512]{1,0:T(8,128)(2,1)} %k.1, bf16[128,512]{1,0:T(8,128)(2,1)} %v.1, f32[2,4,128]{2,1,0:T(4,128)} %bitcast.14, f32[2,4,32]{2,1,0:T(4,128)} %bitcast.15, bf16[448,512]{1,0:T(8,128)(2,1)} %bitcast.12, bf16[8,7168]{1,0:T(8,128)(2,1)} %res.1, ...), custom_call_target="tpu_custom_call" | custom-call | tf_op jit(solution)/shard_map/layer/pallas_call | solution.py:729
  128.5 1.6 %copy.15 = bf16[8,7168]{1,0:T(8,128)(2,1)} copy(bf16[8,7168]{1,0:T(8,128)(2,1)} %layer.1) | data formatting | bytes 229376
